TPU v7x, 32 devices: a whole 2x2x4 slice. The times are simulated.
32 devices in a mesh: wide: 8 (over z, x), narrow: 4 (over y, core).
Axes of the slice: x: 2, y: 2, z: 4, core: 2. Of those that a mesh axis runs over, the one named last changes fastest.
Arguments:
- tokens: bfloat16 [32768, 768], P(('wide', 'narrow')), may hold values from -6 to 6
- qkv_weight: float32 [768, 2304], P('wide', 'narrow'), may hold values from -0.875 to 0.875
- qv_bias: float32 [1536], P(('wide', 'narrow')), may hold values from -3 to 3
- out_weight: float32 [768, 768], P('wide', 'narrow'), may hold values from -2 to 2
- out_bias: float32 [768], P(('wide', 'narrow')), may hold values from -4 to 4
- up_weight: float32 [768, 3072], P('wide', 'narrow'), may hold values from -0.21875 to 0.21875
- up_bias: float32 [3072], P(('wide', 'narrow')), may hold values from -3 to 3
- down_weight: float32 [3072, 768], P('wide', 'narrow'), may hold values from -0.875 to 0.875
- down_bias: float32 [768], P(('wide', 'narrow')), may hold values from -4 to 4
- norm1_gain: float32 [768], P(('wide', 'narrow')), may hold values from 0.5 to 1.5
- norm1_bias: float32 [768], P(('wide', 'narrow')), may hold values from -2 to 2
- norm2_gain: float32 [768], P(('wide', 'narrow')), may hold values from 0.5 to 1.5
- norm2_bias: float32 [768], P(('wide', 'narrow')), may hold values from -2 to 2
- lengths: int32 [32, 2], P(('wide', 'narrow')), may hold values from 0 to 1024, as said below
- cotangent: bfloat16 [32768, 768], P(('wide', 'narrow')), may hold values from -6 to 6
Outputs:
- output: bfloat16 [32768, 768], P(('wide', 'narrow'))
- grad_tokens: bfloat16 [32768, 768], P(('wide', 'narrow'))
- grad_qkv_weight: float32 [768, 2304], P('wide', 'narrow')
- grad_qv_bias: float32 [1536], P(('wide', 'narrow'))
- grad_out_weight: float32 [768, 768], P('wide', 'narrow')
- grad_out_bias: float32 [768], P(('wide', 'narrow'))
- grad_up_weight: float32 [768, 3072], P('wide', 'narrow')
- grad_up_bias: float32 [3072], P(('wide', 'narrow'))
- grad_down_weight: float32 [3072, 768], P('wide', 'narrow')
- grad_down_bias: float32 [768], P(('wide', 'narrow'))
- grad_norm1_gain: float32 [768], P(('wide', 'narrow'))
- grad_norm1_bias: float32 [768], P(('wide', 'narrow'))
- grad_norm2_gain: float32 [768], P(('wide', 'narrow'))
- grad_norm2_bias: float32 [768], P(('wide', 'narrow'))
Inputs may be any that keep to these rules, and one draw needn't show every extreme that they name: `lengths`: each device row holds either one sequence of 1024 tokens (second length 0), two of 512, or one of 1024 / 2 (second length 0); some device holds 1024 tokens.
All inputs are finite; a program needn't handle non-finite values.
Results may differ from a plain program's by a relative error of at most 0.015.
The roundings to bfloat16 on the way count: a program that leaves them out, or rounds other values in their place, can miss the bound.
Values may be sent and summed in bfloat16 or wider, within the bound.
No kernel may reach another device: no remote copies, remote signals or barrier semaphores. Data moves between devices by JAX's collectives and lax.ppermute only.
A program may use at most 256 MiB of HBM per device.

v0:
```python
import jax
import jax.numpy as jnp
import numpy as np
from jax import lax
from jax.experimental import pallas as pl
from jax.experimental.pallas import tpu as pltpu
from jax.sharding import PartitionSpec as P

HEADS = 12
BOTH = ("wide", "narrow")
bf16 = jnp.bfloat16
f32 = jnp.float32
epsilon = 1e-05
branch_scale = 24 ** (-0.5)
D = 768
FF = 3072
HD = 64
ROWS = 1024
QB = 256
NEG = -1e30
UNIT = (48, 128)
SMALL = (
    ("qv", 0, 48, 2),
    ("outb", 48, 24, 1),
    ("downb", 72, 24, 1),
    ("gain1", 96, 24, 1),
    ("shift1", 128, 24, 1),
    ("gain2", 152, 24, 1),
    ("shift2", 176, 24, 1),
    ("upb", 256, 96, 4),
)
ROW_OF = {}
_row = 0
for _name, _off, _wd, _n in SMALL:
    ROW_OF[_name] = _row
    _row += _n
VECS = 16


def nn(a, b):
    return lax.dot_general(a, b, (((1,), (0,)), ((), ())), preferred_element_type=f32)


def nt(a, b):
    return lax.dot_general(a, b, (((1,), (1,)), ((), ())), preferred_element_type=f32)


def normalize(values):
    average = jnp.mean(values, axis=-1, keepdims=True)
    centred = values - average
    spread = jnp.mean(centred * centred, axis=-1, keepdims=True)
    rinv = lax.rsqrt(spread + epsilon)
    return centred * rinv, rinv


def params(flops, bytes_accessed):
    return dict(
        compiler_params=pltpu.CompilerParams(vmem_limit_bytes=60 * 1024 * 1024),
        cost_estimate=pl.CostEstimate(
            flops=int(flops), transcendentals=0, bytes_accessed=int(bytes_accessed)
        ),
    )


VM = pl.BlockSpec(memory_space=pltpu.VMEM)
SM = pl.BlockSpec(memory_space=pltpu.SMEM)
HB = pl.BlockSpec(memory_space=pl.ANY)


def sds(shape, dtype):
    return jax.ShapeDtypeStruct(shape, dtype)


def over_rows(body, blocks=ROWS // QB):
    def step(r, carry):
        body(pl.ds(pl.multiple_of(r * QB, QB), QB), r)
        return carry

    lax.fori_loop(0, blocks, step, 0)


def wait(ref, sem):
    pltpu.make_async_copy(ref, ref, sem).wait()


def lanes(ref, count):
    return jnp.concatenate([ref[g].reshape(D, 128) for g in range(count)], axis=1)


def held_by(meta, q, k, own):
    w, n = meta[0], meta[1]
    z, x, y, c = w // 2, w % 2, n // 2, n % 2
    core = c if own else 1 - c
    first, second = q % 2, q // 2
    dx = jnp.where(core == 0, first, second)
    dy = jnp.where(core == 0, second, first)
    zz = z ^ k
    return zz * 2 + (x ^ dx), core, y ^ dy


def piece_loop(meta, quads, issue):
    for own in (True, False):
        for q in range(4):
            ref = quads[q if own else 4 + q]
            for k in range(4):
                i, core, y = held_by(meta, q, k, own)
                issue(ref.at[k], i, core, y)


def place_loop(pieces, meta, own, other, issue):
    if pieces:
        for mine, ref in ((True, own), (False, other)):
            for q in range(4):
                for k in range(4):
                    i, core, y = held_by(meta, q, k, mine)
                    issue(ref.at[q, k], i, core, y)
    else:
        for i in range(8):
            for n in range(4):
                issue(own.at[i, n], i, n % 2, n // 2)


def places(pieces, units):
    if pieces:
        return (sds((4, 4, units) + UNIT, bf16), sds((4, 4, units) + UNIT, bf16))
    return (sds((8, 4, units) + UNIT, bf16), sds((8, 128), bf16))


def small_map(off, wd, row):
    lane = lax.broadcasted_iota(jnp.int32, (128, D), 1) + row * D
    within = lane - wd * jnp.floor((lane.astype(f32) + 0.5) * (1.0 / wd)).astype(jnp.int32)
    src = lax.broadcasted_iota(jnp.int32, (128, D), 0)
    return jnp.where(src == within + off % 128, 1.0, 0.0).astype(bf16)


def unpack_small(packed):
    rows = []
    for _, off, wd, count in SMALL:
        base = off // 128 * 16
        group = packed[:, base : base + 16, :].astype(f32)[:, 0, :].astype(bf16)
        for row in range(count):
            spread = nn(group, small_map(off, wd, row))
            lane = lax.broadcasted_iota(jnp.int32, (32, D), 1) + row * D
            low = lax.broadcasted_iota(jnp.int32, (32, D), 0) * wd
            keep = (lane >= low) & (lane < low + wd)
            rows.append(jnp.sum(jnp.where(keep, spread, 0.0), axis=0, keepdims=True))
    rows.append(jnp.zeros((VECS - len(rows), D), f32))
    return jnp.concatenate(rows, axis=0)


def pack_small(vec_row):
    groups = [jnp.zeros((32, 128), f32) for _ in range(3)]
    for name, off, wd, count in SMALL:
        for row in range(count):
            lane = lax.broadcasted_iota(jnp.int32, (32, D), 1) + row * D
            low = lax.broadcasted_iota(jnp.int32, (32, D), 0) * wd
            keep = (lane >= low) & (lane < low + wd)
            spread = jnp.where(keep, vec_row(ROW_OF[name] + row), 0.0).astype(bf16)
            groups[off // 128] += nt(spread, small_map(off, wd, row))
    return groups


def attend_rows(far, get, put):
    lane = lax.broadcasted_iota(jnp.int32, (QB, 128), 1)
    causal = lax.broadcasted_iota(jnp.int32, (QB, QB), 1) <= lax.broadcasted_iota(
        jnp.int32, (QB, QB), 0
    )
    for j in range(ROWS // QB):
        size = QB * (j + 1)
        q = get(0, QB * j, QB)
        outs, logs = [], []
        for h in range(2):
            mine = (lane < HD) if h == 0 else (lane >= HD)
            s = nt(jnp.where(mine, q, jnp.zeros_like(q)), get(1, 0, size))
            parts = []
            if j >= 2:
                parts.append(s[:, :512] + far)
                if j == 3:
                    parts.append(s[:, 512:768])
            elif j == 1:
                parts.append(s[:, :QB])
            parts.append(jnp.where(causal, s[:, size - QB :], NEG))
            s = jnp.concatenate(parts, axis=1)
            top = jnp.max(s, axis=1, keepdims=True)
            e = jnp.exp(s - top)
            total = jnp.sum(e, axis=1, keepdims=True)
            outs.append(nn(e.astype(bf16), get(2, 0, size)) * (1.0 / total))
            logs.append(top + jnp.log(total))
        put(QB * j, jnp.where(lane < HD, outs[0], outs[1]).astype(bf16), jnp.where(lane == 0, logs[0], logs[1]).T[:8])


def front_body(pieces, third, meta, lens, *refs):
    count = 8 if pieces else 1
    if third == 0:
        tok, quads, refs = refs[0], refs[1 : 1 + count], refs[1 + count :]
        if not pieces:
            vec_i, refs = refs[0], refs[1:]
        a1, a1t_o, vec, *refs = refs
    else:
        a1, vec, quads, refs = refs[0], refs[1], refs[2 : 2 + count], refs[2 + count :]
    qkv_o, o_o, lse_o, wq, packed, sem, sem2 = refs
    if pieces:

        def issue(ref, i, core, y):
            pltpu.make_async_copy(
                ref.at[pl.ds(3 * third, 3)], wq.at[pl.ds(3 * y, 3), 2 * i + core], sem
            ).start()
            if third == 0:
                pltpu.make_async_copy(ref.at[9], packed.at[i * 4 + 2 * y + core], sem2).start()

        piece_loop(meta, quads, issue)
    else:
        pltpu.make_async_copy(quads[0], wq, sem).start()
    if third == 0:
        if pieces:
            wait(packed, sem2)
            vec[...] = unpack_small(packed[...])
        else:
            vec[...] = vec_i[...]
        def first_norm(at, r):
            n1, _ = normalize(tok[at, :].astype(f32))
            a1[at, :] = (
                n1 * vec[ROW_OF["gain1"] : ROW_OF["gain1"] + 1, :]
                + vec[ROW_OF["shift1"] : ROW_OF["shift1"] + 1, :]
            ).astype(bf16)

        over_rows(first_norm)
        a1t_o[...] = a1[...].T
    wait(wq, sem)
    bias = []
    for g, row in ((0, 0), (1, 0), (4, 1), (5, 1)):
        lane = 128 * (third + 3 * (g % 2))
        bias.append(vec[ROW_OF["qv"] + row : ROW_OF["qv"] + row + 1, lane : lane + 128])
    zero = jnp.zeros((1, 128), f32)
    bias = jnp.concatenate([bias[0], bias[1], zero, zero, bias[2], bias[3]], axis=1)
    weights = lanes(wq, 6)

    def projection(at, r):
        block = (nn(a1[at, :], weights) + bias).astype(bf16)
        for g in range(6):
            part = block[:, 128 * g : 128 * g + 128]
            qkv_o[g, at, :] = part * jnp.asarray(1.0 / HD, bf16) if g < 2 else part

    over_rows(projection)
    far = jnp.where(lens[0, 0] < ROWS, NEG, 0.0).astype(f32)

    def one(pair, carry):
        def put(row, o, lse):
            o_o[pair, row : row + QB, :] = o
            lse_o[pair, :, row : row + QB] = lse

        attend_rows(far, lambda which, row, n: qkv_o[2 * which + pair, row : row + n, :], put)
        return carry

    lax.fori_loop(0, 2, one, 0)


def front(pieces, third, meta, lens, first, vec, weights):
    shapes = [
        sds((6, ROWS, 128), bf16),
        sds((2, ROWS, 128), bf16),
        sds((2, 8, ROWS), f32),
        sds((6, 16) + UNIT, bf16),
    ]
    if third == 0:
        shapes = [sds((ROWS, D), bf16), sds((D, ROWS), bf16), sds((VECS, D), f32)] + shapes
        args = (first,) + tuple(weights) + (() if pieces else (vec,))
        specs = [VM] + [HB] * len(weights) + ([] if pieces else [VM])
    else:
        args = (first, vec) + tuple(weights)
        specs = [VM, VM] + [HB] * len(weights)
    return pl.pallas_call(
        lambda *refs: front_body(pieces, third, *refs),
        out_shape=tuple(shapes),
        in_specs=[SM, SM] + specs,
        out_specs=(VM,) * len(shapes),
        scratch_shapes=[
            pltpu.VMEM((32,) + UNIT, bf16),
            pltpu.SemaphoreType.DMA(()),
            pltpu.SemaphoreType.DMA(()),
        ],
        name=f"front_{third}",
        **params(20e9 if third == 0 else 13e9, 8e6),
    )(meta, lens, *args)


ROW_DN, ROW_G2, ROW_B2, ROW_OB, ROW_UP = 0, 1, 2, 3, 4


def middle_body(pieces, meta, lens, tok, o_0, o_1, o_2, cot, vec, *refs):
    count = 8 if pieces else 3
    quads, refs = refs[:count], refs[count:]
    out_o, dh_o, do_o, own_a, other_a, own_b, other_b, sums_o = refs[:8]
    (
        wo, wup, wdn, h_s, a2_s, a2t_s, dm_s, dmt_s, m_s, da2_s, gl_s, dz_s, st_u, st_d, st_o, upb_s,
        sem_w, sem_m, sem_o, sem_p,
    ) = refs[8:]
    if pieces:

        def issue(ref, i, core, y):
            n = 2 * y + core
            pltpu.make_async_copy(
                ref.at[pl.ds(24, 3)], wo.at[pl.ds(3 * y, 3), 2 * i + core], sem_w
            ).start()
            for third in range(3):
                base = 8 * third
                for half in range(2):
                    pltpu.make_async_copy(
                        ref.at[pl.ds(base + 2 * half, 2)],
                        wup.at[third, 2 * n + half, pl.ds(2 * i, 2)],
                        sem_m,
                    ).start()
                pltpu.make_async_copy(
                    ref.at[pl.ds(base + 4, 4)], wdn.at[third, i, pl.ds(4 * n, 4)], sem_m
                ).start()

        piece_loop(meta, quads, issue)
    else:
        pltpu.make_async_copy(quads[0], wo, sem_w).start()
        pltpu.make_async_copy(quads[1], wup, sem_m).start()
        pltpu.make_async_copy(quads[2], wdn, sem_m).start()
    total = lens[0, 0] + lens[0, 1]
    row_of = lambda name: vec[ROW_OF[name] : ROW_OF[name] + 1, :]
    gain2, shift2, outb, downb = (row_of(n) for n in ("gain2", "shift2", "outb", "downb"))
    for t in range(3):
        upb_s[t : t + 1, :] = jnp.concatenate(
            [
                vec[
                    ROW_OF["upb"] + i // 2 : ROW_OF["upb"] + i // 2 + 1,
                    384 * (i % 2) + 128 * t : 384 * (i % 2) + 128 * t + 128,
                ]
                for i in range(8)
            ],
            axis=1,
        )
    sums_o[...] = jnp.zeros_like(sums_o)

    def attended(at):
        return jnp.concatenate([ref[p, at, :] for p in range(2) for ref in (o_0, o_1, o_2)], axis=1)

    wait(wo, sem_w)
    w_out = lanes(wo, 6)

    def prologue(at, r):
        h = tok[at, :].astype(f32) + branch_scale * (nn(attended(at), w_out) + outb)
        h_s[at, :] = h
        n2, _ = normalize(h)
        a2_s[at, :] = (n2 * gain2 + shift2).astype(bf16)
        live = (lax.broadcasted_iota(jnp.int32, (QB, D), 0) + QB * r) < total
        dm = (branch_scale * jnp.where(live, cot[at, :].astype(f32), 0.0)).astype(bf16)
        dm_s[at, :] = dm
        sums_o[ROW_DN : ROW_DN + 1, :D] += jnp.sum(dm.astype(f32), axis=0, keepdims=True)

    over_rows(prologue)
    a2t_s[...] = a2_s[...].T
    dmt_s[...] = dm_s[...].T
    m_s[...] = jnp.zeros_like(m_s)
    da2_s[...] = jnp.zeros_like(da2_s)
    wait(wup, sem_m)
    wait(wdn, sem_m)
    c0 = 0.7978845608028654
    c1 = 0.044715 * c0

    def emit(own, other, base):
        def issue(ref, i, core, y):
            n = 2 * y + core
            for half in range(2):
                pltpu.make_async_copy(
                    st_u.at[2 * n + half, pl.ds(2 * i, 2)], ref.at[pl.ds(base + 2 * half, 2)], sem_o
                ).start()
            pltpu.make_async_copy(
                st_d.at[i, pl.ds(4 * n, 4)], ref.at[pl.ds(base + 4, 4)], sem_o
            ).start()

        place_loop(pieces, meta, own, other, issue)

    def step(t, carry):
        up = lanes(wup.at[t], 8)
        dn = lanes(wdn.at[t], 8)
        bup = upb_s[pl.ds(t, 1), :]
        sums_o[pl.ds(ROW_UP + t, 1), :] = jnp.zeros((1, 1024), f32)

        def some(r, carry):
            at = pl.ds(pl.multiple_of(r * 256, 256), 256)
            z = nn(a2_s[at, :], up) + bup
            dgl = nn(dm_s[at, :], dn)
            zz = z * z
            th = jnp.tanh(z * (c0 + c1 * zz))
            half = 0.5 * th + 0.5
            gl = (z * half).astype(bf16)
            slope = half + (0.5 * z) * (1.0 - th * th) * (c0 + (3.0 * c1) * zz)
            dz = (dgl * slope).astype(bf16)
            gl_s[at, :] = gl
            dz_s[at, :] = dz
            sums_o[pl.ds(ROW_UP + t, 1), :] += jnp.sum(dz.astype(f32), axis=0, keepdims=True)
            m_s[at, :] += nt(gl, dn)
            da2_s[at, :] += nt(dz, up)
            return carry

        lax.fori_loop(0, 4, some, 0)

        @pl.when(t >= 1)
        def _():
            wait(st_u, sem_o)
            wait(st_d, sem_o)


        def some_rows(r, carry):
            at = pl.ds(pl.multiple_of(r * 384, 128), 384)
            for to, left, right in ((st_u, a2t_s, dz_s), (st_d, dmt_s, gl_s)):
                grad = nn(left[at, :], right[...]).astype(bf16)
                for b in range(8):
                    to[b, pl.ds(8 * r, 8)] = grad[:, 128 * b : 128 * b + 128].reshape((8,) + UNIT)
            return carry

        lax.fori_loop(0, 2, some_rows, 0)

        @pl.when(t == 0)
        def _():
            emit(own_a, other_a, 0)

        @pl.when(t == 1)
        def _():
            emit(own_a, other_a, 8)

        @pl.when(t == 2)
        def _():
            emit(own_b, other_b, 0)

        return carry

    lax.fori_loop(0, 3, step, 0)

    def epilogue(at, r):
        h = h_s[at, :]
        out_o[at, :] = (h + branch_scale * (m_s[at, :] + downb)).astype(bf16)
        n2, r2 = normalize(h)
        da2 = da2_s[at, :]
        sums_o[ROW_G2 : ROW_G2 + 1, :D] += jnp.sum(da2 * n2, axis=0, keepdims=True)
        sums_o[ROW_B2 : ROW_B2 + 1, :D] += jnp.sum(da2, axis=0, keepdims=True)
        e = da2 * gain2
        live = (lax.broadcasted_iota(jnp.int32, (QB, D), 0) + QB * r) < total
        dy = jnp.where(live, cot[at, :].astype(f32), 0.0)
        dh = dy + r2 * (
            e
            - jnp.mean(e, axis=-1, keepdims=True)
            - n2 * jnp.mean(e * n2, axis=-1, keepdims=True)
        )
        dh_o[at, :] = dh
        du = (branch_scale * dh).astype(bf16)
        sums_o[ROW_OB : ROW_OB + 1, :D] += jnp.sum(du.astype(f32), axis=0, keepdims=True)
        dm_s[at, :] = du
        do = nt(du, w_out).astype(bf16)
        for g in range(6):
            do_o[g, at, :] = do[:, 128 * g : 128 * g + 128]

    over_rows(epilogue)
    a2t_s[...] = attended(pl.ds(0, ROWS)).T
    grad = nn(a2t_s[...], dm_s[...])
    for g in range(6):
        st_o[g] = grad[:, 128 * g : 128 * g + 128].astype(bf16).reshape((16,) + UNIT)

    def issue_out(ref, i, core, y):
        pltpu.make_async_copy(
            st_o.at[pl.ds(3 * y, 3), 2 * i + core], ref.at[pl.ds(8, 3)], sem_p
        ).start()

    place_loop(pieces, meta, own_b, other_b, issue_out)
    wait(st_u, sem_o)
    wait(st_d, sem_o)
    wait(st_o, sem_p)


def middle(pieces, meta, lens, tokens, attended, cotangent, vec, weights):
    block = (16,) + UNIT
    return pl.pallas_call(
        lambda *refs: middle_body(pieces, *refs),
        out_shape=(
            sds((ROWS, D), bf16),
            sds((ROWS, D), f32),
            sds((6, ROWS, 128), bf16),
            *places(pieces, 16),
            *places(pieces, 11),
            sds((8, 1024), f32),
        ),
        in_specs=[SM, SM, VM, VM, VM, VM, VM, VM] + [HB] * len(weights),
        out_specs=(VM, VM, VM, HB, HB, HB, HB, VM),
        scratch_shapes=[
            pltpu.VMEM((6,) + block, bf16),
            pltpu.VMEM((3, 8) + block, bf16),
            pltpu.VMEM((3, 8) + block, bf16),
            pltpu.VMEM((ROWS, D), f32),
            pltpu.VMEM((ROWS, D), bf16),
            pltpu.VMEM((D, ROWS), bf16),
            pltpu.VMEM((ROWS, D), bf16),
            pltpu.VMEM((D, ROWS), bf16),
            pltpu.VMEM((ROWS, D), f32),
            pltpu.VMEM((ROWS, D), f32),
            pltpu.VMEM((ROWS, 1024), bf16),
            pltpu.VMEM((ROWS, 1024), bf16),
            pltpu.VMEM((8,) + block, bf16),
            pltpu.VMEM((8,) + block, bf16),
            pltpu.VMEM((6,) + block, bf16),
            pltpu.VMEM((8, 1024), f32),
            pltpu.SemaphoreType.DMA(()),
            pltpu.SemaphoreType.DMA(()),
            pltpu.SemaphoreType.DMA(()),
            pltpu.SemaphoreType.DMA(()),
        ],
        name="middle",
        **params(60e9, 40e6),
    )(meta, lens, tokens, *attended, cotangent, vec, *weights)


def back_pair(far, q_ref, k_ref, v_ref, do_ref, lse_ref, out, pair, dk_s, dv_s):
    lane = lax.broadcasted_iota(jnp.int32, (QB, 128), 1)
    causal = lax.broadcasted_iota(jnp.int32, (QB, QB), 0) <= lax.broadcasted_iota(
        jnp.int32, (QB, QB), 1
    )
    kt = k_ref[...].T
    sub = lax.broadcasted_iota(jnp.int32, (128, ROWS), 0)
    dk_s[...] = jnp.zeros_like(dk_s)
    dv_s[...] = jnp.zeros_like(dv_s)
    for j in range(ROWS // QB):
        size = QB * (j + 1)
        q = q_ref[QB * j : size, :]
        do = do_ref[QB * j : size, :]
        dq = jnp.zeros((128, QB), f32)
        dk = jnp.zeros((size, 128), f32)
        dv = jnp.zeros((size, 128), f32)
        for h in range(2):
            mine = (lane < HD) if h == 0 else (lane >= HD)
            qh = jnp.where(mine, q, jnp.zeros_like(q))
            doh = jnp.where(mine, do, jnp.zeros_like(do))
            s = nt(k_ref[:size, :], qh)
            parts = []
            if j >= 2:
                parts.append(s[:512] + far)
                if j == 3:
                    parts.append(s[512:768])
            elif j == 1:
                parts.append(s[:QB])
            parts.append(jnp.where(causal, s[size - QB :], NEG))
            s = jnp.concatenate(parts, axis=0)
            p = jnp.exp(s - lse_ref[h : h + 1, QB * j : size])
            dp = nt(v_ref[:size, :], doh)
            dot = jnp.sum(p * dp, axis=0, keepdims=True)
            ds = (p * (dp - dot)).astype(bf16)
            dv += nn(p.astype(bf16), doh)
            dk += nn(ds, qh)
            keep = (sub < HD) if h == 0 else (sub >= HD)
            dq += nn(jnp.where(keep, kt, jnp.zeros_like(kt))[:, :size], ds)
        out[pair, QB * j : size, :] = (dq.T * (1.0 / HD)).astype(bf16)
        dk_s[:size, :] += dk
        dv_s[:size, :] += dv
    out[2 + pair] = dk_s[...].astype(bf16)
    out[4 + pair] = dv_s[...].astype(bf16)


def back_body(pieces, third, meta, lens, qkv, do, lse, a1t, wq, vec, *refs):
    if third > 0:
        refs = refs[2:]
    if third == 2:
        mid, sums_0, sums_1, *refs = refs
    dqkv_o, own, other, sums_o, dk_s, dv_s, st, st_v, sem, sem2 = refs
    far = jnp.where(lens[0, 0] < ROWS, NEG, 0.0).astype(f32)

    def one(pair, carry):
        back_pair(
            far, qkv.at[pair], qkv.at[2 + pair], qkv.at[4 + pair], do.at[third + 3 * pair], lse.at[pair],
            dqkv_o, pair, dk_s, dv_s,
        )
        return carry

    lax.fori_loop(0, 2, one, 0)
    raw = jnp.zeros((D, 128), f32)
    plain = jnp.zeros((D, 128), f32)
    cols = []
    for two in range(3):
        blocks = nn(a1t[...], jnp.concatenate([dqkv_o[2 * two], dqkv_o[2 * two + 1]], axis=1))
        for g in (2 * two, 2 * two + 1):
            block = blocks[:, 128 * (g % 2) : 128 * (g % 2) + 128]
            col = jnp.sum(dqkv_o[g].astype(f32), axis=0, keepdims=True)
            cols.append(col)
            st[g] = block.astype(bf16).reshape((16,) + UNIT)
            weight = wq[g].reshape(D, 128).astype(f32)
            raw += block * weight
            plain += weight * col
    base = 3 * third

    def issue(ref, i, core, y):
        pltpu.make_async_copy(
            st.at[pl.ds(3 * y, 3), 2 * i + core], ref.at[pl.ds(base, 3)], sem
        ).start()

    place_loop(pieces, meta, own, other, issue)
    raw = jnp.sum(raw, axis=1, keepdims=True)
    plain = jnp.sum(plain, axis=1, keepdims=True)
    lane = lax.broadcasted_iota(jnp.int32, (D, 128), 1)
    flat = jnp.where(lane == 0, raw, plain).T[:8]
    sums = jnp.concatenate([jnp.concatenate(cols, axis=1), flat[:2], jnp.zeros((5, D), f32)], axis=0)
    sums_o[...] = sums
    if third == 2:
        per = [sums_0[...], sums_1[...], sums]
        raw = per[0][1:2] + per[1][1:2] + per[2][1:2]
        shift = per[0][2:3] + per[1][2:3] + per[2][2:3]
        row_of = lambda name: vec[ROW_OF[name] : ROW_OF[name] + 1, :]
        gain = (raw - row_of("shift1") * shift) / row_of("gain1")
        pick = lambda g: jnp.concatenate(
            [per[p % 3][0:1, 128 * (g + p // 3) : 128 * (g + p // 3) + 128] for p in range(6)], axis=1
        )
        known = {
            "outb": mid[ROW_OB : ROW_OB + 1, :D],
            "downb": mid[ROW_DN : ROW_DN + 1, :D],
            "gain1": gain,
            "shift1": shift,
            "gain2": mid[ROW_G2 : ROW_G2 + 1, :D],
            "shift2": mid[ROW_B2 : ROW_B2 + 1, :D],
        }
        rows = {ROW_OF["qv"]: pick(0), ROW_OF["qv"] + 1: pick(4)}
        for name, value in known.items():
            rows[ROW_OF[name]] = value
        for r in range(4):
            rows[ROW_OF["upb"] + r] = jnp.concatenate(
                [
                    mid[ROW_UP + t : ROW_UP + t + 1, 128 * i : 128 * i + 128]
                    for i in (2 * r, 2 * r + 1)
                    for t in range(3)
                ],
                axis=1,
            )
        groups = pack_small(lambda r: rows[r])
        for g in range(3):
            st_v[:, 16 * g : 16 * g + 16, :] = jnp.broadcast_to(
                groups[g][:, None, :], (32, 16, 128)
            ).astype(bf16)

        def issue_small(ref, i, core, y):
            pltpu.make_async_copy(st_v.at[i * 4 + 2 * y + core], ref.at[9], sem2).start()

        place_loop(pieces, meta, own, other, issue_small)
        wait(st_v, sem2)
    wait(st, sem)


def back(pieces, third, meta, lens, qkv, do, lse, a1t, wq, vec, before):
    args = [meta, lens, qkv, do, lse, a1t, wq, vec, *before]
    extra = [HB, HB] * (third > 0) + [VM, VM, VM] * (third == 2)
    return pl.pallas_call(
        lambda *refs: back_body(pieces, third, *refs),
        out_shape=(
            sds((6, ROWS, 128), bf16),
            *places(pieces, 10),
            sds((8, D), f32),
        ),
        in_specs=[SM, SM] + [VM] * 6 + extra,
        out_specs=(VM, HB, HB, VM),
        input_output_aliases={8: 1, 9: 2} if third > 0 else {},
        scratch_shapes=[
            pltpu.VMEM((ROWS, 128), f32),
            pltpu.VMEM((ROWS, 128), f32),
            pltpu.VMEM((6, 16) + UNIT, bf16),
            pltpu.VMEM((32,) + UNIT, bf16),
            pltpu.SemaphoreType.DMA(()),
            pltpu.SemaphoreType.DMA(()),
        ],
        name=f"back_{third}",
        **params(18e9, 8e6),
    )(*args)


def first_norm_back_body(tok, d_0, d_1, d_2, w_0, w_1, w_2, dh, vec, *refs):
    gt_o = refs[-1]
    gain1 = vec[ROW_OF["gain1"] : ROW_OF["gain1"] + 1, :]

    def body(at, r):
        da1 = jnp.zeros((QB, D), f32)
        for grad, weight in ((d_0, w_0), (d_1, w_1), (d_2, w_2)):
            rows = jnp.concatenate([grad[g, at, :] for g in range(6)], axis=1)
            da1 += nt(rows, lanes(weight, 6))
        n1, r1 = normalize(tok[at, :].astype(f32))
        e = da1 * gain1
        back = r1 * (
            e
            - jnp.mean(e, axis=-1, keepdims=True)
            - n1 * jnp.mean(e * n1, axis=-1, keepdims=True)
        )
        gt_o[at, :] = (dh[at, :] + back).astype(bf16)

    over_rows(body, 2)


def first_norm_back(half, tokens, grads, weights, dh, vec, before=None):
    count = ROWS // 2
    rows = pl.BlockSpec((count, D), lambda g: (half, 0))
    every = lambda shape: pl.BlockSpec(shape, lambda g: (0,) * len(shape))
    return pl.pallas_call(
        first_norm_back_body,
        grid=(1,),
        out_shape=sds((ROWS, D), bf16),
        in_specs=[rows]
        + [pl.BlockSpec((6, count, 128), lambda g: (0, half, 0))] * 3
        + [every((6, 16) + UNIT)] * 3
        + [rows, every((VECS, D))]
        + ([] if before is None else [HB]),
        out_specs=rows,
        input_output_aliases={} if before is None else {9: 0},
        name=f"first_norm_back_{half}",
        **params(8e9, 9e6),
    )(tokens, *grads, *weights, dh, vec, *(() if before is None else (before,)))


def links(step):
    pairs = []
    for z in range(4):
        for x in range(2):
            for y in range(2):
                for c in range(2):
                    tz, tx, ty, tc = step(z, x, y, c)
                    pairs.append(((z * 2 + x) * 4 + y * 2 + c, (tz * 2 + tx) * 4 + ty * 2 + tc))
    return pairs


TO_CORE = links(lambda z, x, y, c: (z, x, y, 1 - c))
TO_FIRST = links(lambda z, x, y, c: (z, 1 - x, y, c) if c == 0 else (z, x, 1 - y, c))
TO_SECOND = links(lambda z, x, y, c: (z, x, 1 - y, c) if c == 0 else (z, 1 - x, y, c))
TO_Z = [None] + [links(lambda z, x, y, c, k=k: (z ^ k, x, y, c)) for k in (1, 2, 3)]


def send(value, pairs):
    return lax.ppermute(value, BOTH, pairs)


def after(value, *others):
    return lax.optimization_barrier((value, *others))[0]


def add(*parts):
    total = parts[0].astype(f32)
    for part in parts[1:]:
        total = total + part.astype(f32)
    return total


def split(big, sizes):
    out, at = [], 0
    for size in sizes:
        out.append(big[at : at + size])
        at += size
    return out


def as_units(block):
    a, b = block.shape[0] // 48, block.shape[1] // 128
    return block.reshape(a, 48, b, 128).transpose(2, 0, 1, 3).reshape(a * b, 48, 128)


def first_pieces(qkv_weight, out_weight, small):
    core = lax.axis_index("narrow") % 2
    both = jnp.concatenate([qkv_weight, out_weight], axis=1).astype(bf16)
    keep = jnp.where(core == 0, both[:48], both[48:])
    give = jnp.where(core == 0, both[48:], both[:48])
    got = send(give, TO_CORE)
    left = jnp.where(core == 0, keep, got)
    right = jnp.where(core == 0, got, keep)
    cols = as_units(jnp.concatenate([left[:, :576], right[:, :576]], axis=1))
    out = as_units(jnp.concatenate([left[:, 576:], right[:, 576:]], axis=1))
    thirds = [cols[g] for t in range(3) for g in (t, 3 + t, 6 + t)]
    return jnp.concatenate([jnp.stack(thirds), small], axis=0), out


def feed_pieces(up_weight, down_weight):
    up = as_units(up_weight.astype(bf16))
    down = as_units(down_weight.astype(bf16).T)
    out = []
    for t in range(3):
        out.append(jnp.concatenate([up[2 * t : 2 * t + 2], up[6 + 2 * t : 8 + 2 * t], down[4 * t : 4 * t + 4]]))
    return out


def whole(value, dims):
    for axis, dim in dims:
        value = lax.all_gather(value, axis, axis=dim, tiled=True)
    return value


def plain_weights(qkv_weight, out_weight, up_weight, down_weight, vectors):
    matrix = lambda w: whole(w.astype(bf16), (("narrow", 1), ("wide", 0)))
    blocks = lambda w, b: w.reshape(16, 48, b, 128).transpose(2, 0, 1, 3)
    wq = blocks(matrix(qkv_weight), 18)
    wq = [jnp.stack([wq[g] for g in (t, 3 + t, 6 + t, 9 + t, 12 + t, 15 + t)]) for t in range(3)]
    wo = blocks(matrix(out_weight), 6)
    up = blocks(matrix(up_weight), 24).reshape(8, 3, 16, 48, 128).transpose(1, 0, 2, 3, 4)
    down = blocks(matrix(down_weight).T, 24).reshape(8, 3, 16, 48, 128).transpose(1, 0, 2, 3, 4)
    rows = [
        whole(vectors[name].astype(bf16), (("narrow", 0), ("wide", 0))).astype(f32).reshape(count, D)
        for name, _, _, count in SMALL
    ]
    vec = jnp.concatenate(rows + [jnp.zeros((VECS - 12, D), f32)], axis=0)
    return wq, wo, up, down, vec


def plain_grads(q_all, m_a, m_b):
    def reduce(matrix):
        rows = lax.psum_scatter(matrix.astype(f32), "wide", scatter_dimension=0, tiled=True)
        return lax.psum_scatter(rows.astype(bf16), "narrow", scatter_dimension=1, tiled=True).astype(f32)

    def vector(values):
        rows = lax.psum_scatter(values, "wide", scatter_dimension=0, tiled=True)
        return lax.psum_scatter(rows.astype(bf16), "narrow", scatter_dimension=0, tiled=True).astype(f32)

    q = q_all[:, :, :9].reshape(8, 2, 2, 3, 3, 48, 128)
    qkv = q.transpose(0, 2, 5, 1, 4, 3, 6).reshape(D, 2304)
    out = m_b[:, :, 8:].reshape(8, 2, 2, 3, 48, 128).transpose(0, 2, 4, 1, 3, 5).reshape(D, D)
    m = jnp.concatenate([m_a, m_b[:, :, :8]], axis=2).reshape(8, 4, 3, 2, 4, 48, 128)
    up = m[:, :, :, 0].reshape(8, 4, 3, 2, 2, 48, 128).transpose(0, 4, 5, 1, 3, 2, 6).reshape(D, FF)
    down = m[:, :, :, 1].transpose(0, 2, 5, 1, 3, 4).reshape(FF, D)
    small = q_all[:, :, 9].reshape(32, 3, 16, 128)[:, :, 0].reshape(32, 384).astype(f32)
    vecs = {name: vector(small[:, off : off + wd].reshape(-1)) for name, off, wd, _ in SMALL}
    return reduce(qkv), reduce(out), reduce(up), reduce(down), vecs


class Spread:
    def __init__(self, piece, *waits):
        near = send(after(piece, *waits), TO_Z[1])
        self.parts = [piece, near] + [send(piece, TO_Z[k]) for k in (2, 3)]

    def along(self, *waits):
        self.line = after(jnp.stack(self.parts, axis=0), *waits)
        self.first = send(self.line, TO_FIRST)
        self.second = send(self.line, TO_SECOND)

    def across(self, *waits):
        self.corner = send(after(self.first, *waits), TO_SECOND)

    def swap(self, *waits):
        self.swapped = [send(after(part, *waits), TO_CORE) for part in (self.line, self.first, self.second)]

    def end(self, *waits):
        last = send(after(self.corner, *waits), TO_CORE)
        return (self.line, self.first, self.second, self.corner, *self.swapped, last)


class Fold:
    def __init__(self, own, other):
        self.own = own
        self.got = send(other, TO_CORE)

    def second(self, *waits):
        self.got = after(self.got, *waits)
        self.sum_2 = add(self.own[2:], self.got[2:]).astype(bf16)
        self.sec = send(self.sum_2, TO_SECOND)

    def first(self, *waits):
        self.sec = after(self.sec, *waits)
        self.sum_1 = add(self.own[1], self.got[1], self.sec[1]).astype(bf16)
        self.fst = send(self.sum_1, TO_FIRST)

    def line(self, *waits):
        self.fst = after(self.fst, *waits)
        mine = [add(self.own[0, k], self.got[0, k], self.sec[0, k], self.fst[k]) for k in range(4)]
        self.mine = mine[0]
        self.sum_0 = [part.astype(bf16) for part in mine[1:]]
        self.far = [send(part, TO_Z[k + 1]) for k, part in enumerate(self.sum_0)]

    def end(self, *waits):
        return add(self.mine, *(after(part, *waits) for part in self.far))


def joined(blocks):
    return jnp.concatenate(blocks, axis=1)


def fast_grads(q_all, m_a, m_b):
    core = lax.axis_index("narrow") % 2
    m = jnp.concatenate([m_a, m_b[:8]], axis=0).reshape(3, 2, 4, 48, 128)
    grad_up = joined([m[t, 0, 2 * h : 2 * h + 2].reshape(96, 128) for h in range(2) for t in range(3)])
    grad_down = joined([m[t, 1].reshape(192, 128) for t in range(3)]).T
    cols = joined([q_all[3 * t + g] for g in range(3) for t in range(3)])
    outs = joined([m_b[8 + g] for g in range(3)])
    low = joined([cols[:, :576], outs[:, :192]])
    high = joined([cols[:, 576:], outs[:, 192:]])
    keep = jnp.where(core == 0, low, high)
    got = send(jnp.where(core == 0, high, low), TO_CORE)
    rows = jnp.concatenate([jnp.where(core == 0, keep, got), jnp.where(core == 0, got, keep)], axis=0)
    small = q_all[9].reshape(3, 16, 128)[:, 0].reshape(384)
    vecs = {name: small[off : off + wd] for name, off, wd, _ in SMALL}
    return rows[:, :576], rows[:, 576:], grad_up, grad_down, vecs


def local(
    tokens,
    qkv_weight,
    qv_bias,
    out_weight,
    out_bias,
    up_weight,
    up_bias,
    down_weight,
    down_bias,
    norm1_gain,
    norm1_bias,
    norm2_gain,
    norm2_bias,
    lengths,
    cotangent,
    fast,
):
    vectors = {
        "qv": qv_bias,
        "outb": out_bias,
        "downb": down_bias,
        "gain1": norm1_gain,
        "shift1": norm1_bias,
        "gain2": norm2_gain,
        "shift2": norm2_bias,
        "upb": up_bias,
    }
    meta = jnp.stack([lax.axis_index("wide"), lax.axis_index("narrow")]).astype(jnp.int32)
    if fast:
        zeros = lambda size: jnp.zeros((size,), f32)
        small = jnp.concatenate(
            [qv_bias, out_bias, down_bias, norm1_gain, zeros(8)]
            + [norm1_bias, norm2_gain, norm2_bias, zeros(56), up_bias, zeros(32)]
        )
        small = jnp.pad(small.astype(bf16).reshape(3, 1, 128), ((0, 0), (0, 15), (0, 0))).reshape(1, 48, 128)
        piece_q, piece_o = first_pieces(qkv_weight, out_weight, small)
        feed = feed_pieces(up_weight, down_weight)
        heads = Spread(piece_q)
        rest = Spread(jnp.concatenate(feed + [piece_o]), heads.parts[1])
        heads.along(rest.parts[1])
        heads.across(rest.parts[2])
        heads.swap()
        ready = heads.end()
        rest.along(heads.corner)
        first = after(tokens, rest.line)
        a1, a1t, vec, qkv_0, o_0, lse_0, wq_0 = front(True, 0, meta, lengths, first, None, ready)
        qkv_1, o_1, lse_1, wq_1 = front(True, 1, meta, lengths, a1, vec, ready)
        rest.across(o_1)
        rest.swap(o_1)
        qkv_2, o_2, lse_2, wq_2 = front(True, 2, meta, lengths, a1, vec, ready)
        weights = rest.end(o_2)
    else:
        wq, wo, up, down, vec = plain_weights(qkv_weight, out_weight, up_weight, down_weight, vectors)
        a1, a1t, vec, qkv_0, o_0, lse_0, wq_0 = front(False, 0, meta, lengths, tokens, vec, (wq[0],))
        qkv_1, o_1, lse_1, wq_1 = front(False, 1, meta, lengths, a1, vec, (wq[1],))
        qkv_2, o_2, lse_2, wq_2 = front(False, 2, meta, lengths, a1, vec, (wq[2],))
        weights = (wo, up, down)
    output, dh, do, own_a, other_a, own_b, other_b, mid = middle(
        fast, meta, lengths, tokens, (o_0, o_1, o_2), cotangent, vec, weights
    )
    args = lambda qkv, lse, wq: (qkv, do, lse, a1t, wq, vec)
    d_0, own, other, sums_0 = back(fast, 0, meta, lengths, *args(qkv_0, lse_0, wq_0), ())
    if fast:
        ff_a, ff_b = Fold(own_a, other_a), Fold(own_b, other_b)
        ff_a.second(d_0)
        do = after(do, ff_a.sum_2, ff_b.got)
    d_1, own, other, sums_1 = back(fast, 1, meta, lengths, *args(qkv_1, lse_1, wq_1), (own, other))
    if fast:
        ff_b.second(d_1)
        ff_a.first(d_1)
        do = after(do, ff_b.sum_2, ff_a.sum_1)
    d_2, own, other, _ = back(
        fast, 2, meta, lengths, *args(qkv_2, lse_2, wq_2), (own, other, mid, sums_0, sums_1)
    )
    grads, weights = (d_0, d_1, d_2), (wq_0, wq_1, wq_2)
    if fast:
        at = Fold(own, other)
        ff_b.first(d_2)
        dh = after(dh, ff_b.sum_1)
    top = first_norm_back(0, tokens, grads, weights, dh, vec)
    if fast:
        ff_a.line(top)
        at.second(top)
        dh = after(dh, at.sum_2, *ff_a.sum_0)
    grad_tokens = first_norm_back(1, tokens, grads, weights, dh, vec, top)
    if fast:
        at.first(grad_tokens)
        total_a = ff_a.end(at.sum_1)
        ff_b.line(total_a)
        at.line(*ff_b.sum_0)
        g_qkv, g_out, g_up, g_down, vecs = fast_grads(at.end(), total_a, ff_b.end(*at.sum_0))
    else:
        g_qkv, g_out, g_up, g_down, vecs = plain_grads(own, own_a, own_b)
    return (
        output,
        grad_tokens,
        g_qkv,
        vecs["qv"],
        g_out,
        vecs["outb"],
        g_up,
        vecs["upb"],
        g_down,
        vecs["downb"],
        vecs["gain1"],
        vecs["shift1"],
        vecs["gain2"],
        vecs["shift2"],
    )


def solution(mesh):
    fast = mesh.shape["wide"] == 8 and mesh.shape["narrow"] == 4
    rows, matrix, vector = P(BOTH, None), P("wide", "narrow"), P(BOTH)
    return jax.shard_map(
        lambda *args: local(*args, fast),
        mesh=mesh,
        in_specs=(
            rows, matrix, vector, matrix, vector, matrix, vector, matrix, vector,
            vector, vector, vector, vector, rows, rows,
        ),
        out_specs=(
            rows, rows, matrix, vector, matrix, vector, matrix, vector, matrix, vector,
            vector, vector, vector, vector,
        ),
        check_vma=False,
    )
```

profile of v0, /device:TPU:0, one launch (start us, length us, event | category | flops | bytes accessed | tf_op | source)
XLA Modules:
  0.0 310.9 jit_solution(3465264835418951536)
XLA Ops:
  8.5 4.0 %collective-permute-done.1 = bf16[10,48,128]{2,1,0:T(8,128)(2,1)S(1)} collective-permute-done((bf16[10,48,128]{2,1,0:T(8,128)(2,1)S(1)}, bf16[10,48,128]{2,1,0:T(8,128)(2,1)S(1)}, u32[]{:S(2)}, u32[]{:S(2)}) %collective-permute-start.1) | collective-permute-done | bytes 122912 | tf_op jit(solution)/shard_map/ppermute | solution.py:731
  16.8 11.2 %collective-permute-done.6 = bf16[10,48,128]{2,1,0:T(8,128)(2,1)S(1)} collective-permute-done((bf16[10,48,128]{2,1,0:T(8,128)(2,1)S(1)}, bf16[10,48,128]{2,1,0:T(8,128)(2,1)S(1)}, u32[]{:S(2)}, u32[]{:S(2)}) %collective-permute-start.6) | collective-permute-done | bytes 122912 | tf_op jit(solution)/shard_map/ppermute | solution.py:731
  32.9 12.1 %collective-permute-done.3 = bf16[27,48,128]{2,1,0:T(8,128)(2,1)S(1)} collective-permute-done((bf16[27,48,128]{2,1,0:T(8,128)(2,1)S(1)}, bf16[27,48,128]{2,1,0:T(8,128)(2,1)S(1)}, u32[]{:S(2)}, u32[]{:S(2)}) %collective-permute-start.3) | collective-permute-done | bytes 331808 | tf_op jit(solution)/shard_map/ppermute | solution.py:731
  46.1 7.8 %collective-permute-done.8.refs_6_.refs_7_ = bf16[4,10,48,128]{3,2,1,0:T(8,128)(2,1)} collective-permute-done((bf16[4,10,48,128]{3,2,1,0:T(8,128)(2,1)S(1)}, bf16[4,10,48,128]{3,2,1,0:T(8,128)(2,1)}, u32[]{:S(2)}, u32[]{:S(2)}) %collective-permute-start.8) | collective-permute-done | bytes 491552 | tf_op jit(solution)/shard_map/ppermute | solution.py:731
  54.0 3.5 %collective-permute-start.4 = (bf16[27,48,128]{2,1,0:T(8,128)(2,1)S(1)}, bf16[27,48,128]{2,1,0:T(8,128)(2,1)S(1)}, u32[]{:S(2)}, u32[]{:S(2)}) collective-permute-start(bf16[27,48,128]{2,1,0:T(8,128)(2,1)S(1)} %constant_dynamic-update-slice_fusion), channel_id=1, source_target_pairs={{0,24},{1,25},{2,26},{3,27},{4,28},{5,29},{6,30},{7,31},{8,16},{9,... | collective-permute-start | bytes 995336 | tf_op jit(solution)/shard_map/ppermute | solution.py:731
  58.1 8.0 %collective-permute-done.4 = bf16[27,48,128]{2,1,0:T(8,128)(2,1)S(1)} collective-permute-done((bf16[27,48,128]{2,1,0:T(8,128)(2,1)S(1)}, bf16[27,48,128]{2,1,0:T(8,128)(2,1)S(1)}, u32[]{:S(2)}, u32[]{:S(2)}) %collective-permute-start.4) | collective-permute-done | bytes 331808 | tf_op jit(solution)/shard_map/ppermute | solution.py:731
  68.4 15.9 %front_0.1 = (bf16[1024,768]{1,0:T(8,128)(2,1)}, bf16[768,1024]{1,0:T(8,128)(2,1)}, f32[16,768]{1,0:T(8,128)}, bf16[6,1024,128]{2,1,0:T(8,128)(2,1)}, bf16[2,102...) custom-call(s32[2]{0:T(128)} %pad_add_fusion.refs_0_, s32[1,2]{1,0:T(1,128)} %refs_1_.13, ...), custom_call_target="tpu_custom_call" | custom-call | flops 20000000000 | bytes 8000000 | tf_op jit(solution)/shard_map/front_0/pallas_call | solution.py:272
  84.3 12.1 %front_1.1 = (bf16[6,1024,128]{2,1,0:T(8,128)(2,1)}, bf16[2,1024,128]{2,1,0:T(8,128)(2,1)}, f32[2,8,1024]{2,1,0:T(8,128)}, bf16[6,16,48,128]{3,2,1,0:T(8,128)(2,1)}) custom-call(s32[2]{0:T(128)} %pad_add_fusion.refs_0_, s32[1,2]{1,0:T(1,128)} %refs_1_.13, bf16[1024,768]{1,0:T(8,128)(2,1)} %get-tuple-element.82.refs_2_, ...), custom_call_target="tpu_custom_call" | custom-call | flops 12999999488 | bytes 8000000 | tf_op jit(solution)/shard_map/front_1/pallas_call | solution.py:272
  98.3 12.1 %front_2.1 = (bf16[6,1024,128]{2,1,0:T(8,128)(2,1)}, bf16[2,1024,128]{2,1,0:T(8,128)(2,1)}, f32[2,8,1024]{2,1,0:T(8,128)}, bf16[6,16,48,128]{3,2,1,0:T(8,128)(2,1)}) custom-call(s32[2]{0:T(128)} %pad_add_fusion.refs_0_, s32[1,2]{1,0:T(1,128)} %refs_1_.13, bf16[1024,768]{1,0:T(8,128)(2,1)} %get-tuple-element.82.refs_2_, ...), custom_call_target="tpu_custom_call" | custom-call | flops 12999999488 | bytes 8000000 | tf_op jit(solution)/shard_map/front_2/pallas_call | solution.py:272
  111.0 4.3 %collective-permute-done.16.refs_11_ = bf16[4,27,48,128]{3,2,1,0:T(8,128)(2,1)} collective-permute-done((bf16[4,27,48,128]{3,2,1,0:T(8,128)(2,1)}, bf16[4,27,48,128]{3,2,1,0:T(8,128)(2,1)}, u32[]{:S(2)}, u32[]{:S(2)}) %collective-permute-start.16) | collective-permute-done | bytes 1327136 | tf_op jit(solution)/shard_map/ppermute | solution.py:731
  119.6 55.4 %middle.1 = (bf16[1024,768]{1,0:T(8,128)(2,1)}, f32[1024,768]{1,0:T(8,128)}, bf16[6,1024,128]{2,1,0:T(8,128)(2,1)}, bf16[4,4,16,48,128]{4,3,2,1,0:T(8,128)(2,1)}...) custom-call(s32[2]{0:T(128)} %pad_add_fusion.refs_0_, ...), custom_call_target="tpu_custom_call" | custom-call | flops 60000002048 | bytes 40000000 | tf_op jit(solution)/shard_map/middle/pallas_call | solution.py:476
  175.6 14.8 %back_0.1 = (bf16[6,1024,128]{2,1,0:T(8,128)(2,1)}, bf16[4,4,10,48,128]{4,3,2,1,0:T(8,128)(2,1)}, bf16[4,4,10,48,128]{4,3,2,1,0:T(8,128)(2,1)}, f32[8,768]{1,0:T(8,128)}) custom-call(s32[2]{0:T(128)} %pad_add_fusion.refs_0_, s32[1,2]{1,0:T(1,128)} %refs_1_.13, bf16[6,1024,128]{2,1,0:T(8,128)(2,1)} %get-tuple-element.91.refs_2_, ...), custom_call_target="tpu_custom_call" | custom-call | flops 17999998976 | bytes 8000000 | tf_op jit(solution)/shard_map/back_0/pallas_call | solution.py:649
  190.5 3.1 add_convert_fusion
  194.4 14.4 %back_1.1 = (bf16[6,1024,128]{2,1,0:T(8,128)(2,1)}, bf16[4,4,10,48,128]{4,3,2,1,0:T(8,128)(2,1)}, bf16[4,4,10,48,128]{4,3,2,1,0:T(8,128)(2,1)}, f32[8,768]{1,0:T(8,128)}) custom-call(s32[2]{0:T(128)} %pad_add_fusion.refs_0_, s32[1,2]{1,0:T(1,128)} %refs_1_.13, ...), custom_call_target="tpu_custom_call", output_to_operand_aliasing={{1}: (8, {}), {2}: (9, {})} | custom-call | flops 17999998976 | bytes 8000000 | tf_op jit(solution)/shard_map/back_1/pallas_call | solution.py:649
  208.8 2.9 add_convert_fusion.1
  216.8 15.9 %back_2.1 = (bf16[6,1024,128]{2,1,0:T(8,128)(2,1)}, bf16[4,4,10,48,128]{4,3,2,1,0:T(8,128)(2,1)}, bf16[4,4,10,48,128]{4,3,2,1,0:T(8,128)(2,1)}, f32[8,768]{1,0:T(8,128)}) custom-call(s32[2]{0:T(128)} %pad_add_fusion.refs_0_, s32[1,2]{1,0:T(1,128)} %refs_1_.13, ...), custom_call_target="tpu_custom_call", output_to_operand_aliasing={{1}: (8, {}), {2}: (9, {})} | custom-call | flops 17999998976 | bytes 8000000 | tf_op jit(solution)/shard_map/back_2/pallas_call | solution.py:649
  237.4 7.1 %first_norm_back_0.1.refs_0_ = bf16[1024,768]{1,0:T(8,128)(2,1)} custom-call(bf16[1024,768]{1,0:T(8,128)(2,1)} %tok.3, bf16[6,1024,128]{2,1,0:T(8,128)(2,1)} %get-tuple-element.96.d_0, bf16[6,1024,128]{2,1,0:T(8,128)(2,1)} %get-tuple-element.107.d_1, bf16[6,1024,128]{2,1,0:T(8,128)(2,1)} %get-tuple-element.120.d_2, ...), custom_call_target="tpu_custom_call" | custom-call | flops 8000000000 | bytes 9000000 | tf_op jit(solution)/shard_map/first_norm_back_0/pallas_call | solution.py:697
  252.2 3.5 %collective-permute-start.32 = (bf16[16,48,128]{2,1,0:T(8,128)(2,1)}, bf16[16,48,128]{2,1,0:T(8,128)(2,1)}, u32[]{:S(2)}, u32[]{:S(2)}) collective-permute-start(bf16[16,48,128]{2,1,0:T(8,128)(2,1)} %get-tuple-element.140), channel_id=1, source_target_pairs={{0,24},{1,25},{2,26},{3,27},{4,28},{5,29},{6,30},{7,31},{8,16},{9,... | collective-permute-start | bytes 589832 | tf_op jit(solution)/shard_map/ppermute | solution.py:731
  255.7 3.8 %collective-permute-start.31 = (bf16[16,48,128]{2,1,0:T(8,128)(2,1)}, bf16[16,48,128]{2,1,0:T(8,128)(2,1)}, u32[]{:S(2)}, u32[]{:S(2)}) collective-permute-start(bf16[16,48,128]{2,1,0:T(8,128)(2,1)} %get-tuple-element.141), channel_id=1, source_target_pairs={{0,16},{1,17},{2,18},{3,19},{4,20},{5,21},{6,22},{7,23},{8,24},{9,... | collective-permute-start | bytes 589832 | tf_op jit(solution)/shard_map/ppermute | solution.py:731
  259.6 7.0 %first_norm_back_1.1 = bf16[1024,768]{1,0:T(8,128)(2,1)} custom-call(bf16[1024,768]{1,0:T(8,128)(2,1)} %tok.3, bf16[6,1024,128]{2,1,0:T(8,128)(2,1)} %get-tuple-element.96.d_0, bf16[6,1024,128]{2,1,0:T(8,128)(2,1)} %get-tuple-element.107.d_1, bf16[6,1024,128]{2,1,0:T(8,128)(2,1)} %get-tuple-element.120.d_2, ...), custom_call_target="tpu_custom_call", output_to_operand_aliasing={{}: (9, {})} | custom-call | flops 8000000000 | bytes 9000000 | tf_op jit(solution)/shard_map/first_norm_back_1/pallas_call | solution.py:697
  269.2 4.4 %collective-permute-done.31 = bf16[16,48,128]{2,1,0:T(8,128)(2,1)} collective-permute-done((bf16[16,48,128]{2,1,0:T(8,128)(2,1)}, bf16[16,48,128]{2,1,0:T(8,128)(2,1)}, u32[]{:S(2)}, u32[]{:S(2)}) %collective-permute-start.31) | collective-permute-done | bytes 196640 | tf_op jit(solution)/shard_map/ppermute | solution.py:731
  276.9 3.6 %collective-permute-start.38 = (bf16[11,48,128]{2,1,0:T(8,128)(2,1)S(1)}, bf16[11,48,128]{2,1,0:T(8,128)(2,1)S(1)}, u32[]{:S(2)}, u32[]{:S(2)}) collective-permute-start(bf16[11,48,128]{2,1,0:T(8,128)(2,1)S(1)} %get-tuple-element.144), channel_id=1, source_target_pairs={{0,24},{1,25},{2,26},{3,27},{4,28},{5,29},{6,30},{7,31},{8,16},{9,... | collective-permute-start | bytes 405512 | tf_op jit(solution)/shard_map/ppermute | solution.py:731
  282.4 5.4 %collective-permute-done.38 = bf16[11,48,128]{2,1,0:T(8,128)(2,1)S(1)} collective-permute-done((bf16[11,48,128]{2,1,0:T(8,128)(2,1)S(1)}, bf16[11,48,128]{2,1,0:T(8,128)(2,1)S(1)}, u32[]{:S(2)}, u32[]{:S(2)}) %collective-permute-start.38) | collective-permute-done | bytes 135200 | tf_op jit(solution)/shard_map/ppermute | solution.py:731
  299.5 5.6 %collective-permute-done.34 = bf16[10,48,128]{2,1,0:T(8,128)(2,1)S(1)} collective-permute-done((bf16[10,48,128]{2,1,0:T(8,128)(2,1)S(1)}, bf16[10,48,128]{2,1,0:T(8,128)(2,1)S(1)}, u32[]{:S(2)}, u32[]{:S(2)}) %collective-permute-start.34) | collective-permute-done | bytes 122912 | tf_op jit(solution)/shard_map/ppermute | solution.py:731
  (200 shorter events, 71.0 us)
Async XLA Ops:
  12.4 15.6 %collective-permute-start.2 = (bf16[27,48,128]{2,1,0:T(8,128)(2,1)S(1)}, bf16[27,48,128]{2,1,0:T(8,128)(2,1)S(1)}, u32[]{:S(2)}, u32[]{:S(2)}) collective-permute-start(bf16[27,48,128]{2,1,0:T(8,128)(2,1)S(1)} %constant_dynamic-update-slice_fusion), channel_id=1, source_target_pairs={{0,8},{1,9},{2,10},{3,11},{4,12},{5,13},{6,14},{7,15},{8,0},{9,1},... | collective-permute-start | bytes 995336 | tf_op jit(solution)/shard_map/ppermute | solution.py:731
  14.2 13.8 %collective-permute-start.6 = (bf16[10,48,128]{2,1,0:T(8,128)(2,1)S(1)}, bf16[10,48,128]{2,1,0:T(8,128)(2,1)S(1)}, u32[]{:S(2)}, u32[]{:S(2)}) collective-permute-start(bf16[10,48,128]{2,1,0:T(8,128)(2,1)S(1)} %constant_dynamic-update-slice_fusion.10), channel_id=1, source_target_pairs={{0,24},{1,25},{2,26},{3,27},{4,28},{5,29},{6,30},{7,31},{8,16},{9,... | collective-permute-start | bytes 368648 | tf_op jit(solution)/shard_map/ppermute | solution.py:731
  28.0 17.0 %collective-permute-start.7 = (bf16[4,10,48,128]{3,2,1,0:T(8,128)(2,1)S(1)}, bf16[4,10,48,128]{3,2,1,0:T(8,128)(2,1)S(1)}, u32[]{:S(2)}, u32[]{:S(2)}) collective-permute-start(bf16[4,10,48,128]{3,2,1,0:T(8,128)(2,1)S(1)} %pad_maximum_fusion.2.refs_3_.refs_4_), channel_id=1, source_target_pairs={{0,4},{1,3},{2,6},{3,1},{4,0},{5,7},{6,2},{7,5},{8,12},{9,11},{10,... | collective-permute-start | bytes 1474568 | tf_op jit(solution)/shard_map/ppermute | solution.py:731
  29.6 15.4 %collective-permute-start.3 = (bf16[27,48,128]{2,1,0:T(8,128)(2,1)S(1)}, bf16[27,48,128]{2,1,0:T(8,128)(2,1)S(1)}, u32[]{:S(2)}, u32[]{:S(2)}) collective-permute-start(bf16[27,48,128]{2,1,0:T(8,128)(2,1)S(1)} %constant_dynamic-update-slice_fusion), channel_id=1, source_target_pairs={{0,16},{1,17},{2,18},{3,19},{4,20},{5,21},{6,22},{7,23},{8,24},{9,... | collective-permute-start | bytes 995336 | tf_op jit(solution)/shard_map/ppermute | solution.py:731
  31.4 14.2 %collective-permute-start.9 = (bf16[4,10,48,128]{3,2,1,0:T(8,128)(2,1)S(1)}, bf16[4,10,48,128]{3,2,1,0:T(8,128)(2,1)S(1)}, u32[]{:S(2)}, u32[]{:S(2)}) collective-permute-start(bf16[4,10,48,128]{3,2,1,0:T(8,128)(2,1)S(1)} %pad_maximum_fusion.2.refs_3_.refs_4_), channel_id=1, source_target_pairs={{0,2},{1,5},{2,0},{3,7},{4,6},{5,1},{6,4},{7,3},{8,10},{9,13},{10,... | collective-permute-start | bytes 1474568 | tf_op jit(solution)/shard_map/ppermute | solution.py:731
  45.5 21.3 %collective-permute-start.10 = (bf16[4,10,48,128]{3,2,1,0:T(8,128)(2,1)S(1)}, bf16[4,10,48,128]{3,2,1,0:T(8,128)(2,1)}, u32[]{:S(2)}, u32[]{:S(2)}) collective-permute-start(bf16[4,10,48,128]{3,2,1,0:T(8,128)(2,1)S(1)} %pad_maximum_fusion.2.refs_3_.refs_4_), channel_id=1, source_target_pairs={{0,1},{1,0},{2,3},{3,2},{4,5},{5,4},{6,7},{7,6},{8,9},{9,8},{10,11... | collective-permute-start | bytes 1474568 | tf_op jit(solution)/shard_map/ppermute | solution.py:731
  45.6 22.8 %collective-permute-start.12 = (bf16[4,10,48,128]{3,2,1,0:T(8,128)(2,1)S(1)}, bf16[4,10,48,128]{3,2,1,0:T(8,128)(2,1)}, u32[]{:S(2)}, u32[]{:S(2)}) collective-permute-start(bf16[4,10,48,128]{3,2,1,0:T(8,128)(2,1)S(1)} %collective-permute-done.9.refs_5_.refs_6_), channel_id=1, source_target_pairs={{0,1},{1,0},{2,3},{3,2},{4,5},{5,4},{6,7},{7,6},{8,9},{9,8},{10,11... | collective-permute-start | bytes 1474568 | tf_op jit(solution)/shard_map/ppermute | solution.py:731
  46.1 22.3 %collective-permute-start.11 = (bf16[4,10,48,128]{3,2,1,0:T(8,128)(2,1)S(1)}, bf16[4,10,48,128]{3,2,1,0:T(8,128)(2,1)}, u32[]{:S(2)}, u32[]{:S(2)}) collective-permute-start(bf16[4,10,48,128]{3,2,1,0:T(8,128)(2,1)S(1)} %collective-permute-done.7.refs_4_.refs_5_), channel_id=1, source_target_pairs={{0,1},{1,0},{2,3},{3,2},{4,5},{5,4},{6,7},{7,6},{8,9},{9,8},{10,11... | collective-permute-start | bytes 1474568 | tf_op jit(solution)/shard_map/ppermute | solution.py:731
  54.0 14.4 %collective-permute-start.13 = (bf16[4,10,48,128]{3,2,1,0:T(8,128)(2,1)}, bf16[4,10,48,128]{3,2,1,0:T(8,128)(2,1)}, u32[]{:S(2)}, u32[]{:S(2)}) collective-permute-start(bf16[4,10,48,128]{3,2,1,0:T(8,128)(2,1)} %collective-permute-done.8.refs_6_.refs_7_), channel_id=1, source_target_pairs={{0,1},{1,0},{2,3},{3,2},{4,5},{5,4},{6,7},{7,6},{8,9},{9,8},{10,11... | collective-permute-start | bytes 1474568 | tf_op jit(solution)/shard_map/ppermute | solution.py:731
  66.3 44.4 %collective-permute-start.15 = (bf16[4,27,48,128]{3,2,1,0:T(8,128)(2,1)S(1)}, bf16[4,27,48,128]{3,2,1,0:T(8,128)(2,1)S(1)}, u32[]{:S(2)}, u32[]{:S(2)}) collective-permute-start(bf16[4,27,48,128]{3,2,1,0:T(8,128)(2,1)S(1)} %pad_maximum_fusion.refs_8_), channel_id=1, source_target_pairs={{0,2},{1,5},{2,0},{3,7},{4,6},{5,1},{6,4},{7,3},{8,10},{9,13},{10,... | collective-permute-start | bytes 3981320 | tf_op jit(solution)/shard_map/ppermute | solution.py:731
  66.9 30.3 %collective-permute-start.14 = (bf16[4,27,48,128]{3,2,1,0:T(8,128)(2,1)S(1)}, bf16[4,27,48,128]{3,2,1,0:T(8,128)(2,1)}, u32[]{:S(2)}, u32[]{:S(2)}) collective-permute-start(bf16[4,27,48,128]{3,2,1,0:T(8,128)(2,1)S(1)} %pad_maximum_fusion.refs_8_), channel_id=1, source_target_pairs={{0,4},{1,3},{2,6},{3,1},{4,0},{5,7},{6,2},{7,5},{8,12},{9,11},{10,... | collective-permute-start | bytes 3981320 | tf_op jit(solution)/shard_map/ppermute | solution.py:731
  97.1 18.1 %collective-permute-start.16 = (bf16[4,27,48,128]{3,2,1,0:T(8,128)(2,1)}, bf16[4,27,48,128]{3,2,1,0:T(8,128)(2,1)}, u32[]{:S(2)}, u32[]{:S(2)}) collective-permute-start(bf16[4,27,48,128]{3,2,1,0:T(8,128)(2,1)} %collective-permute-done.14.refs_9_), channel_id=1, source_target_pairs={{0,2},{1,5},{2,0},{3,7},{4,6},{5,1},{6,4},{7,3},{8,10},{9,13},{10,... | collective-permute-start | bytes 3981320 | tf_op jit(solution)/shard_map/ppermute | solution.py:731
  98.0 17.4 %collective-permute-start.17 = (bf16[4,27,48,128]{3,2,1,0:T(8,128)(2,1)S(1)}, bf16[4,27,48,128]{3,2,1,0:T(8,128)(2,1)}, u32[]{:S(2)}, u32[]{:S(2)}) collective-permute-start(bf16[4,27,48,128]{3,2,1,0:T(8,128)(2,1)S(1)} %pad_maximum_fusion.refs_8_), channel_id=1, source_target_pairs={{0,1},{1,0},{2,3},{3,2},{4,5},{5,4},{6,7},{7,6},{8,9},{9,8},{10,11... | collective-permute-start | bytes 3981320 | tf_op jit(solution)/shard_map/ppermute | solution.py:731
  175.0 15.4 %collective-permute-start.21 = (bf16[4,4,16,48,128]{4,3,2,1,0:T(8,128)(2,1)}, bf16[4,4,16,48,128]{4,3,2,1,0:T(8,128)(2,1)}, u32[]{:S(2)}, u32[]{:S(2)}) collective-permute-start(bf16[4,4,16,48,128]{4,3,2,1,0:T(8,128)(2,1)} %get-tuple-element.99), channel_id=1, source_target_pairs={{0,1},{1,0},{2,3},{3,2},{4,5},{5,4},{6,7},{7,6},{8,9},{9,8},{10,11... | collective-permute-start | bytes 9437192 | tf_op jit(solution)/shard_map/ppermute | solution.py:731
  175.2 19.2 %collective-permute-start.22 = (bf16[4,4,11,48,128]{4,3,2,1,0:T(8,128)(2,1)}, bf16[4,4,11,48,128]{4,3,2,1,0:T(8,128)(2,1)}, u32[]{:S(2)}, u32[]{:S(2)}) collective-permute-start(bf16[4,4,11,48,128]{4,3,2,1,0:T(8,128)(2,1)} %get-tuple-element.101), channel_id=1, source_target_pairs={{0,1},{1,0},{2,3},{3,2},{4,5},{5,4},{6,7},{7,6},{8,9},{9,8},{10,11... | collective-permute-start | bytes 6488072 | tf_op jit(solution)/shard_map/ppermute | solution.py:731
  193.5 20.7 %collective-permute-start.23 = (bf16[2,4,16,48,128]{4,3,2,1,0:T(8,128)(2,1)}, bf16[2,4,16,48,128]{4,3,2,1,0:T(8,128)(2,1)}, u32[]{:S(2)}, u32[]{:S(2)}) collective-permute-start(bf16[2,4,16,48,128]{4,3,2,1,0:T(8,128)(2,1)} %add_convert_fusion), channel_id=1, source_target_pairs={{0,2},{1,5},{2,0},{3,7},{4,6},{5,1},{6,4},{7,3},{8,10},{9,13},{10,... | collective-permute-start | bytes 4718600 | tf_op jit(solution)/shard_map/ppermute | solution.py:731
  211.7 22.7 %collective-permute-start.24 = (bf16[2,4,11,48,128]{4,3,2,1,0:T(8,128)(2,1)}, bf16[2,4,11,48,128]{4,3,2,1,0:T(8,128)(2,1)}, u32[]{:S(2)}, u32[]{:S(2)}) collective-permute-start(bf16[2,4,11,48,128]{4,3,2,1,0:T(8,128)(2,1)} %add_convert_fusion.1), channel_id=1, source_target_pairs={{0,2},{1,5},{2,0},{3,7},{4,6},{5,1},{6,4},{7,3},{8,10},{9,13},{10,... | collective-permute-start | bytes 3244040 | tf_op jit(solution)/shard_map/ppermute | solution.py:731
  236.9 38.3 %collective-permute-start.29 = (bf16[4,11,48,128]{3,2,1,0:T(8,128)(2,1)}, bf16[4,11,48,128]{3,2,1,0:T(8,128)(2,1)}, u32[]{:S(2)}, u32[]{:S(2)}) collective-permute-start(bf16[4,11,48,128]{3,2,1,0:T(8,128)(2,1)} %fusion.1), channel_id=1, source_target_pairs={{0,4},{1,3},{2,6},{3,1},{4,0},{5,7},{6,2},{7,5},{8,12},{9,11},{10,... | collective-permute-start | bytes 1622024 | tf_op jit(solution)/shard_map/ppermute | solution.py:731
  248.7 17.8 %collective-permute-start.27 = (bf16[2,4,10,48,128]{4,3,2,1,0:T(8,128)(2,1)}, bf16[2,4,10,48,128]{4,3,2,1,0:T(8,128)(2,1)S(1)}, u32[]{:S(2)}, u32[]{:S(2)}) collective-permute-start(bf16[2,4,10,48,128]{4,3,2,1,0:T(8,128)(2,1)} %add_convert_fusion.2), channel_id=1, source_target_pairs={{0,2},{1,5},{2,0},{3,7},{4,6},{5,1},{6,4},{7,3},{8,10},{9,13},{10,... | collective-permute-start | bytes 2949128 | tf_op jit(solution)/shard_map/ppermute | solution.py:731
  252.2 17.0 %collective-permute-start.32 = (bf16[16,48,128]{2,1,0:T(8,128)(2,1)}, bf16[16,48,128]{2,1,0:T(8,128)(2,1)}, u32[]{:S(2)}, u32[]{:S(2)}) collective-permute-start(bf16[16,48,128]{2,1,0:T(8,128)(2,1)} %get-tuple-element.140), channel_id=1, source_target_pairs={{0,24},{1,25},{2,26},{3,27},{4,28},{5,29},{6,30},{7,31},{8,16},{9,... | collective-permute-start | bytes 589832 | tf_op jit(solution)/shard_map/ppermute | solution.py:731
  255.7 17.9 %collective-permute-start.31 = (bf16[16,48,128]{2,1,0:T(8,128)(2,1)}, bf16[16,48,128]{2,1,0:T(8,128)(2,1)}, u32[]{:S(2)}, u32[]{:S(2)}) collective-permute-start(bf16[16,48,128]{2,1,0:T(8,128)(2,1)} %get-tuple-element.141), channel_id=1, source_target_pairs={{0,16},{1,17},{2,18},{3,19},{4,20},{5,21},{6,22},{7,23},{8,24},{9,... | collective-permute-start | bytes 589832 | tf_op jit(solution)/shard_map/ppermute | solution.py:731
  259.6 14.1 %collective-permute-start.30 = (bf16[16,48,128]{2,1,0:T(8,128)(2,1)}, bf16[16,48,128]{2,1,0:T(8,128)(2,1)}, u32[]{:S(2)}, u32[]{:S(2)}) collective-permute-start(bf16[16,48,128]{2,1,0:T(8,128)(2,1)} %get-tuple-element.142), channel_id=1, source_target_pairs={{0,8},{1,9},{2,10},{3,11},{4,12},{5,13},{6,14},{7,15},{8,0},{9,1},... | collective-permute-start | bytes 589832 | tf_op jit(solution)/shard_map/ppermute | solution.py:731
  268.0 13.1 %collective-permute-start.28 = (bf16[4,10,48,128]{3,2,1,0:T(8,128)(2,1)S(1)}, bf16[4,10,48,128]{3,2,1,0:T(8,128)(2,1)S(1)}, u32[]{:S(2)}, u32[]{:S(2)}) collective-permute-start(bf16[4,10,48,128]{3,2,1,0:T(8,128)(2,1)S(1)} %fusion.2), channel_id=1, source_target_pairs={{0,4},{1,3},{2,6},{3,1},{4,0},{5,7},{6,2},{7,5},{8,12},{9,11},{10,... | collective-permute-start | bytes 1474568 | tf_op jit(solution)/shard_map/ppermute | solution.py:731
  276.8 13.3 %collective-permute-start.37 = (bf16[11,48,128]{2,1,0:T(8,128)(2,1)S(1)}, bf16[11,48,128]{2,1,0:T(8,128)(2,1)S(1)}, u32[]{:S(2)}, u32[]{:S(2)}) collective-permute-start(bf16[11,48,128]{2,1,0:T(8,128)(2,1)S(1)} %get-tuple-element.143), channel_id=1, source_target_pairs={{0,16},{1,17},{2,18},{3,19},{4,20},{5,21},{6,22},{7,23},{8,24},{9,... | collective-permute-start | bytes 405512 | tf_op jit(solution)/shard_map/ppermute | solution.py:731
  (36 other events, 311.0 us)
where the time goes:
time: 315 us; the launch traced here: 311 us
  Pallas kernels  155 us (49%)
  waiting for transfers between devices  73.4 us (23%)
  starting transfers between devices  43.8 us (14%)
  other arithmetic  31.1 us (10%)
  local copies, waits for them, and re-layouts  5.82 us (2%)
    ppermute x40, waiting for transfers between devices, send(): return lax.ppermute(value, BOTH, pairs)  73.4 us
    pallas_call x1, Pallas kernels, middle(): pl.pallas_call(lambda *refs: middle_body(pieces, *refs), out_shape=(sds((...  55.4 us
    pallas_call x3, Pallas kernels, back(): pl.pallas_call(lambda *refs: back_body(pieces, third, *refs), out_shape=(...  45.2 us
    ppermute x40, starting transfers between devices, send(): return lax.ppermute(value, BOTH, pairs)  43.8 us
    pallas_call x3, Pallas kernels, front(): pl.pallas_call(lambda *refs: front_body(pieces, third, *refs), out_shape=...  40.1 us
    pallas_call x2, Pallas kernels, first_norm_back(): pl.pallas_call(first_norm_back_body, grid=(1,), out_shape=sds((ROWS, D),...  14.1 us
    convert_element_type x3, other arithmetic, second(): self.sum_2 = add(self.own[2:], self.got[2:]).astype(bf16)  8.67 us
    convert_element_type x3, other arithmetic, first(): self.sum_1 = add(self.own[1], self.got[1], self.sec[1]).astype(bf16)  6.38 us
  transfers between devices with their start and end apart: 40, of which 17 were waited for; matrix products, arithmetic and copies ran while one was open for 8% of the time, Pallas kernels for 32%

commit v1 on v0

--- a/solution.py
+++ b/solution.py
@@ -53,9 +53,9 @@
     return centred * rinv, rinv
 
 
-def params(flops, bytes_accessed):
+def params(flops, bytes_accessed, mib=60):
     return dict(
-        compiler_params=pltpu.CompilerParams(vmem_limit_bytes=60 * 1024 * 1024),
+        compiler_params=pltpu.CompilerParams(vmem_limit_bytes=mib * 1024 * 1024),
         cost_estimate=pl.CostEstimate(
             flops=int(flops), transcendentals=0, bytes_accessed=int(bytes_accessed)
         ),
@@ -280,7 +280,7 @@
             pltpu.SemaphoreType.DMA(()),
         ],
         name=f"front_{third}",
-        **params(20e9 if third == 0 else 13e9, 8e6),
+        **params(6e9, 8e6, 20),
     )(meta, lens, *args)
 
 
@@ -288,37 +288,28 @@
 
 
 def middle_body(pieces, meta, lens, tok, o_0, o_1, o_2, cot, vec, *refs):
-    count = 8 if pieces else 3
+    count = 8 if pieces else 2
     quads, refs = refs[:count], refs[count:]
     out_o, dh_o, do_o, own_a, other_a, own_b, other_b, sums_o = refs[:8]
     (
-        wo, wup, wdn, h_s, a2_s, a2t_s, dm_s, dmt_s, m_s, da2_s, gl_s, dz_s, st_u, st_d, st_o, upb_s,
+        wo, feed, h_s, a2_s, a2t_s, dm_s, dmt_s, m_s, da2_s, gl_s, dz_s, st, st_o, upb_s,
         sem_w, sem_m, sem_o, sem_p,
     ) = refs[8:]
     if pieces:
 
-        def issue(ref, i, core, y):
-            n = 2 * y + core
+        def issue_out_weight(ref, i, core, y):
             pltpu.make_async_copy(
                 ref.at[pl.ds(24, 3)], wo.at[pl.ds(3 * y, 3), 2 * i + core], sem_w
             ).start()
-            for third in range(3):
-                base = 8 * third
-                for half in range(2):
-                    pltpu.make_async_copy(
-                        ref.at[pl.ds(base + 2 * half, 2)],
-                        wup.at[third, 2 * n + half, pl.ds(2 * i, 2)],
-                        sem_m,
-                    ).start()
-                pltpu.make_async_copy(
-                    ref.at[pl.ds(base + 4, 4)], wdn.at[third, i, pl.ds(4 * n, 4)], sem_m
-                ).start()
-
-        piece_loop(meta, quads, issue)
+
+        def issue_feed(ref, i, core, y):
+            pltpu.make_async_copy(ref.at[pl.ds(0, 24)], feed.at[2 * y + core, i], sem_m).start()
+
+        piece_loop(meta, quads, issue_out_weight)
+        piece_loop(meta, quads, issue_feed)
     else:
         pltpu.make_async_copy(quads[0], wo, sem_w).start()
-        pltpu.make_async_copy(quads[1], wup, sem_m).start()
-        pltpu.make_async_copy(quads[2], wdn, sem_m).start()
+        pltpu.make_async_copy(quads[1], feed, sem_m).start()
     total = lens[0, 0] + lens[0, 1]
     row_of = lambda name: vec[ROW_OF[name] : ROW_OF[name] + 1, :]
     gain2, shift2, outb, downb = (row_of(n) for n in ("gain2", "shift2", "outb", "downb"))
@@ -356,27 +347,24 @@
     dmt_s[...] = dm_s[...].T
     m_s[...] = jnp.zeros_like(m_s)
     da2_s[...] = jnp.zeros_like(da2_s)
-    wait(wup, sem_m)
-    wait(wdn, sem_m)
+    wait(feed, sem_m)
     c0 = 0.7978845608028654
     c1 = 0.044715 * c0
 
     def emit(own, other, base):
         def issue(ref, i, core, y):
-            n = 2 * y + core
-            for half in range(2):
-                pltpu.make_async_copy(
-                    st_u.at[2 * n + half, pl.ds(2 * i, 2)], ref.at[pl.ds(base + 2 * half, 2)], sem_o
-                ).start()
-            pltpu.make_async_copy(
-                st_d.at[i, pl.ds(4 * n, 4)], ref.at[pl.ds(base + 4, 4)], sem_o
-            ).start()
+            pltpu.make_async_copy(st.at[2 * y + core, i], ref.at[pl.ds(base, 8)], sem_o).start()
 
         place_loop(pieces, meta, own, other, issue)
 
     def step(t, carry):
-        up = lanes(wup.at[t], 8)
-        dn = lanes(wdn.at[t], 8)
+        up = jnp.concatenate(
+            [feed[n, :, pl.ds(8 * t + 2 * h, 2)].reshape(D, 128) for n in range(4) for h in range(2)],
+            axis=1,
+        )
+        dn = jnp.concatenate(
+            [feed[:, i, pl.ds(8 * t + 4, 4)].reshape(D, 128) for i in range(8)], axis=1
+        )
         bup = upb_s[pl.ds(t, 1), :]
         sums_o[pl.ds(ROW_UP + t, 1), :] = jnp.zeros((1, 1024), f32)
 
@@ -401,19 +389,17 @@
 
         @pl.when(t >= 1)
         def _():
-            wait(st_u, sem_o)
-            wait(st_d, sem_o)
-
-
-        def some_rows(r, carry):
-            at = pl.ds(pl.multiple_of(r * 384, 128), 384)
-            for to, left, right in ((st_u, a2t_s, dz_s), (st_d, dmt_s, gl_s)):
-                grad = nn(left[at, :], right[...]).astype(bf16)
-                for b in range(8):
-                    to[b, pl.ds(8 * r, 8)] = grad[:, 128 * b : 128 * b + 128].reshape((8,) + UNIT)
-            return carry
-
-        lax.fori_loop(0, 2, some_rows, 0)
+            wait(st, sem_o)
+
+
+        for n in range(4):
+            at = pl.ds(256 * n, 256)
+            grad = nn(a2t_s[...], dz_s[:, at]).astype(bf16)
+            for h in range(2):
+                st[n, :, 2 * h : 2 * h + 2] = grad[:, 128 * h : 128 * h + 128].reshape((8, 2) + UNIT)
+            grad = nn(dmt_s[...], gl_s[:, at]).astype(bf16)
+            for h in range(2):
+                st[:, 2 * n + h, 4:8] = grad[:, 128 * h : 128 * h + 128].reshape((4, 4) + UNIT)
 
         @pl.when(t == 0)
         def _():
@@ -466,8 +452,7 @@
         ).start()
 
     place_loop(pieces, meta, own_b, other_b, issue_out)
-    wait(st_u, sem_o)
-    wait(st_d, sem_o)
+    wait(st, sem_o)
     wait(st_o, sem_p)
 
 
@@ -487,8 +472,7 @@
         out_specs=(VM, VM, VM, HB, HB, HB, HB, VM),
         scratch_shapes=[
             pltpu.VMEM((6,) + block, bf16),
-            pltpu.VMEM((3, 8) + block, bf16),
-            pltpu.VMEM((3, 8) + block, bf16),
+            pltpu.VMEM((4, 8, 24) + UNIT, bf16),
             pltpu.VMEM((ROWS, D), f32),
             pltpu.VMEM((ROWS, D), bf16),
             pltpu.VMEM((D, ROWS), bf16),
@@ -498,8 +482,7 @@
             pltpu.VMEM((ROWS, D), f32),
             pltpu.VMEM((ROWS, 1024), bf16),
             pltpu.VMEM((ROWS, 1024), bf16),
-            pltpu.VMEM((8,) + block, bf16),
-            pltpu.VMEM((8,) + block, bf16),
+            pltpu.VMEM((4, 8, 8) + UNIT, bf16),
             pltpu.VMEM((6,) + block, bf16),
             pltpu.VMEM((8, 1024), f32),
             pltpu.SemaphoreType.DMA(()),
@@ -508,7 +491,7 @@
             pltpu.SemaphoreType.DMA(()),
         ],
         name="middle",
-        **params(60e9, 40e6),
+        **params(60e9, 40e6, 50),
     )(meta, lens, tokens, *attended, cotangent, vec, *weights)
 
 
@@ -665,7 +648,7 @@
             pltpu.SemaphoreType.DMA(()),
         ],
         name=f"back_{third}",
-        **params(18e9, 8e6),
+        **params(18e9, 8e6, 20),
     )(*args)
 
 
@@ -706,7 +689,7 @@
         out_specs=rows,
         input_output_aliases={} if before is None else {9: 0},
         name=f"first_norm_back_{half}",
-        **params(8e9, 9e6),
+        **params(8e9, 9e6, 14),
     )(tokens, *grads, *weights, dh, vec, *(() if before is None else (before,)))
 
 
@@ -790,14 +773,16 @@
     wq = blocks(matrix(qkv_weight), 18)
     wq = [jnp.stack([wq[g] for g in (t, 3 + t, 6 + t, 9 + t, 12 + t, 15 + t)]) for t in range(3)]
     wo = blocks(matrix(out_weight), 6)
-    up = blocks(matrix(up_weight), 24).reshape(8, 3, 16, 48, 128).transpose(1, 0, 2, 3, 4)
-    down = blocks(matrix(down_weight).T, 24).reshape(8, 3, 16, 48, 128).transpose(1, 0, 2, 3, 4)
+    up = blocks(matrix(up_weight), 24).reshape(4, 2, 3, 8, 2, 48, 128)
+    up = up.transpose(0, 3, 2, 1, 4, 5, 6).reshape(4, 8, 3, 4, 48, 128)
+    down = blocks(matrix(down_weight).T, 24).reshape(8, 3, 4, 4, 48, 128).transpose(2, 0, 1, 3, 4, 5)
+    feed = jnp.concatenate([up, down], axis=3).reshape(4, 8, 24, 48, 128)
     rows = [
         whole(vectors[name].astype(bf16), (("narrow", 0), ("wide", 0))).astype(f32).reshape(count, D)
         for name, _, _, count in SMALL
     ]
     vec = jnp.concatenate(rows + [jnp.zeros((VECS - 12, D), f32)], axis=0)
-    return wq, wo, up, down, vec
+    return wq, wo, feed, vec
 
 
 def plain_grads(q_all, m_a, m_b):
@@ -941,11 +926,11 @@
         qkv_2, o_2, lse_2, wq_2 = front(True, 2, meta, lengths, a1, vec, ready)
         weights = rest.end(o_2)
     else:
-        wq, wo, up, down, vec = plain_weights(qkv_weight, out_weight, up_weight, down_weight, vectors)
+        wq, wo, feed, vec = plain_weights(qkv_weight, out_weight, up_weight, down_weight, vectors)
         a1, a1t, vec, qkv_0, o_0, lse_0, wq_0 = front(False, 0, meta, lengths, tokens, vec, (wq[0],))
         qkv_1, o_1, lse_1, wq_1 = front(False, 1, meta, lengths, a1, vec, (wq[1],))
         qkv_2, o_2, lse_2, wq_2 = front(False, 2, meta, lengths, a1, vec, (wq[2],))
-        weights = (wo, up, down)
+        weights = (wo, feed)
     output, dh, do, own_a, other_a, own_b, other_b, mid = middle(
         fast, meta, lengths, tokens, (o_0, o_1, o_2), cotangent, vec, weights
     )

time: 315 us -> 286 us (0.908)
  other arithmetic: 31.1 us -> 9.85 us
  Pallas kernels: 155 us -> 134 us
  waiting for transfers between devices: 73.4 us -> 86.1 us
    ppermute x40, waiting for transfers between devices: 73.4 us -> 86.1 us  [send(): return lax.ppermute(value, BOTH, pairs)]
    convert_element_type x3, other arithmetic: 8.67 us -> 0.96 us  [second(): self.sum_2 = add(self.own[2:], self.got[2:]).astype(bf16)]
    pallas_call x3, Pallas kernels: 45.2 us -> 38.3 us  [back(): pl.pallas_call(lambda *refs: back_body(pieces, third, *refs), out_shape=(...]
    pallas_call x2, Pallas kernels: 14.1 us -> 7.82 us  [first_norm_back(): pl.pallas_call(first_norm_back_body, grid=(1,), out_shape=sds((ROWS, D),...]
    convert_element_type x3, other arithmetic: 6.38 us -> 0.72 us  [first(): self.sum_1 = add(self.own[1], self.got[1], self.sec[1]).astype(bf16)]
    convert_element_type x3, other arithmetic: 5.64 us -> 0.72 us  [line(): self.sum_0 = [part.astype(bf16) for part in mine[1:]]]
    pallas_call x3, Pallas kernels: 40.1 us -> 35.8 us  [front(): pl.pallas_call(lambda *refs: front_body(pieces, third, *refs), out_shape=...]
    add x3, other arithmetic: 3.81 us -> 0.41 us  [add(): total = total + part.astype(f32)]
  transfers between devices with their start and end apart: 40 -> 40, of which waited for: 17 -> 18; matrix products, arithmetic and copies ran while one was open for 8% -> 2% of each run, Pallas kernels for 32% -> 29%
where the time goes in v1:
time: 286 us; the launch traced here: 282 us
  Pallas kernels  134 us (47%)
  waiting for transfers between devices  86.1 us (30%)
  starting transfers between devices  43.6 us (15%)
  other arithmetic  9.85 us (3%)
  local copies, waits for them, and re-layouts  6.79 us (2%)
    ppermute x40, waiting for transfers between devices, send(): return lax.ppermute(value, BOTH, pairs)  86.1 us
    pallas_call x1, Pallas kernels, middle(): pl.pallas_call(lambda *refs: middle_body(pieces, *refs), out_shape=(sds((...  52.3 us
    ppermute x40, starting transfers between devices, send(): return lax.ppermute(value, BOTH, pairs)  43.6 us
    pallas_call x3, Pallas kernels, back(): pl.pallas_call(lambda *refs: back_body(pieces, third, *refs), out_shape=(...  38.3 us
    pallas_call x3, Pallas kernels, front(): pl.pallas_call(lambda *refs: front_body(pieces, third, *refs), out_shape=...  35.8 us
    pallas_call x2, Pallas kernels, first_norm_back(): pl.pallas_call(first_norm_back_body, grid=(1,), out_shape=sds((ROWS, D),...  7.82 us
  transfers between devices with their start and end apart: 40, of which 18 were waited for; matrix products, arithmetic and copies ran while one was open for 2% of the time, Pallas kernels for 29%

profile of v1, /device:TPU:0, one launch (start us, length us, event | category | flops | bytes accessed | tf_op | source)
XLA Modules:
  0.0 282.4 jit_solution(17188963545202137564)
XLA Ops:
  8.5 4.0 %collective-permute-done.1 = bf16[10,48,128]{2,1,0:T(8,128)(2,1)S(1)} collective-permute-done((bf16[10,48,128]{2,1,0:T(8,128)(2,1)S(1)}, bf16[10,48,128]{2,1,0:T(8,128)(2,1)S(1)}, u32[]{:S(2)}, u32[]{:S(2)}) %collective-permute-start.1) | collective-permute-done | bytes 122912 | tf_op jit(solution)/shard_map/ppermute | solution.py:714
  16.7 11.2 %collective-permute-done.6 = bf16[10,48,128]{2,1,0:T(8,128)(2,1)S(1)} collective-permute-done((bf16[10,48,128]{2,1,0:T(8,128)(2,1)S(1)}, bf16[10,48,128]{2,1,0:T(8,128)(2,1)S(1)}, u32[]{:S(2)}, u32[]{:S(2)}) %collective-permute-start.6) | collective-permute-done | bytes 122912 | tf_op jit(solution)/shard_map/ppermute | solution.py:714
  32.9 12.1 %collective-permute-done.3 = bf16[27,48,128]{2,1,0:T(8,128)(2,1)S(1)} collective-permute-done((bf16[27,48,128]{2,1,0:T(8,128)(2,1)S(1)}, bf16[27,48,128]{2,1,0:T(8,128)(2,1)S(1)}, u32[]{:S(2)}, u32[]{:S(2)}) %collective-permute-start.3) | collective-permute-done | bytes 331808 | tf_op jit(solution)/shard_map/ppermute | solution.py:714
  45.6 3.5 %collective-permute-start.4 = (bf16[27,48,128]{2,1,0:T(8,128)(2,1)S(1)}, bf16[27,48,128]{2,1,0:T(8,128)(2,1)S(1)}, u32[]{:S(2)}, u32[]{:S(2)}) collective-permute-start(bf16[27,48,128]{2,1,0:T(8,128)(2,1)S(1)} %constant_dynamic-update-slice_fusion), channel_id=1, source_target_pairs={{0,24},{1,25},{2,26},{3,27},{4,28},{5,29},{6,30},{7,31},{8,16},{9,... | collective-permute-start | bytes 995336 | tf_op jit(solution)/shard_map/ppermute | solution.py:714
  50.1 4.1 %collective-permute-done.8.refs_6_.refs_7_ = bf16[4,10,48,128]{3,2,1,0:T(8,128)(2,1)} collective-permute-done((bf16[4,10,48,128]{3,2,1,0:T(8,128)(2,1)}, bf16[4,10,48,128]{3,2,1,0:T(8,128)(2,1)}, u32[]{:S(2)}, u32[]{:S(2)}) %collective-permute-start.8) | collective-permute-done | bytes 491552 | tf_op jit(solution)/shard_map/ppermute | solution.py:714
  54.2 3.7 %collective-permute-done.4 = bf16[27,48,128]{2,1,0:T(8,128)(2,1)S(1)} collective-permute-done((bf16[27,48,128]{2,1,0:T(8,128)(2,1)S(1)}, bf16[27,48,128]{2,1,0:T(8,128)(2,1)S(1)}, u32[]{:S(2)}, u32[]{:S(2)}) %collective-permute-start.4) | collective-permute-done | bytes 331808 | tf_op jit(solution)/shard_map/ppermute | solution.py:714
  60.3 14.1 %front_0.1 = (bf16[1024,768]{1,0:T(8,128)(2,1)S(1)}, bf16[768,1024]{1,0:T(8,128)(2,1)S(1)}, f32[16,768]{1,0:T(8,128)S(1)}, bf16[6,1024,128]{2,1,0:T(8,128)(2,1)S...) custom-call(s32[2]{0:T(128)S(1)} %pad_add_fusion.refs_0_, ...), custom_call_target="tpu_custom_call" | custom-call | flops 6000000000 | bytes 8000000 | tf_op jit(solution)/shard_map/front_0/pallas_call | solution.py:272
  74.4 11.0 %front_1.1 = (bf16[6,1024,128]{2,1,0:T(8,128)(2,1)S(1)}, bf16[2,1024,128]{2,1,0:T(8,128)(2,1)S(1)}, f32[2,8,1024]{2,1,0:T(8,128)S(1)}, bf16[6,16,48,128]{3,2,1,0:T(8,128)(2,1)S(1)}) custom-call(s32[2]{0:T(128)S(1)} %pad_add_fusion.refs_0_, s32[1,2]{1,0:T(1,128)S(1)} %copy-done.2, bf16[1024,768]{1,0:T(8,128)(2,1)S(1)} %get-tuple-element.82.refs_2_, ...), custom_call_target="tpu_custom_call" | custom-call | flops 6000000000 | bytes 8000000 | tf_op jit(solution)/shard_map/front_1/pallas_call | solution.py:272
  85.3 4.8 %collective-permute-done.14.refs_9_ = bf16[4,27,48,128]{3,2,1,0:T(8,128)(2,1)} collective-permute-done((bf16[4,27,48,128]{3,2,1,0:T(8,128)(2,1)S(1)}, bf16[4,27,48,128]{3,2,1,0:T(8,128)(2,1)}, u32[]{:S(2)}, u32[]{:S(2)}) %collective-permute-start.14) | collective-permute-done | bytes 1327136 | tf_op jit(solution)/shard_map/ppermute | solution.py:714
  91.6 10.8 %front_2.1 = (bf16[6,1024,128]{2,1,0:T(8,128)(2,1)S(1)}, bf16[2,1024,128]{2,1,0:T(8,128)(2,1)S(1)}, f32[2,8,1024]{2,1,0:T(8,128)S(1)}, bf16[6,16,48,128]{3,2,1,0:T(8,128)(2,1)S(1)}) custom-call(s32[2]{0:T(128)S(1)} %pad_add_fusion.refs_0_, s32[1,2]{1,0:T(1,128)S(1)} %copy-done.2, bf16[1024,768]{1,0:T(8,128)(2,1)S(1)} %get-tuple-element.82.refs_2_, ...), custom_call_target="tpu_custom_call" | custom-call | flops 6000000000 | bytes 8000000 | tf_op jit(solution)/shard_map/front_2/pallas_call | solution.py:272
  103.0 5.1 %collective-permute-done.16.refs_11_ = bf16[4,27,48,128]{3,2,1,0:T(8,128)(2,1)S(1)} collective-permute-done((bf16[4,27,48,128]{3,2,1,0:T(8,128)(2,1)}, bf16[4,27,48,128]{3,2,1,0:T(8,128)(2,1)S(1)}, u32[]{:S(2)}, u32[]{:S(2)}) %collective-permute-start.16) | collective-permute-done | bytes 1327136 | tf_op jit(solution)/shard_map/ppermute | solution.py:714
  112.3 52.3 %middle.1 = (bf16[1024,768]{1,0:T(8,128)(2,1)}, f32[1024,768]{1,0:T(8,128)}, bf16[6,1024,128]{2,1,0:T(8,128)(2,1)}, bf16[4,4,16,48,128]{4,3,2,1,0:T(8,128)(2,1)}...) custom-call(s32[2]{0:T(128)S(1)} %pad_add_fusion.refs_0_, ...), custom_call_target="tpu_custom_call" | custom-call | flops 60000002048 | bytes 40000000 | tf_op jit(solution)/shard_map/middle/pallas_call | solution.py:461
  168.0 11.8 %back_0.1 = (bf16[6,1024,128]{2,1,0:T(8,128)(2,1)S(1)}, bf16[4,4,10,48,128]{4,3,2,1,0:T(8,128)(2,1)S(1)}, bf16[4,4,10,48,128]{4,3,2,1,0:T(8,128)(2,1)S(1)}, f32[8,768]{1,0:T(8,128)S(1)}) custom-call(s32[2]{0:T(128)S(1)} %pad_add_fusion.refs_0_, s32[1,2]{1,0:T(1,128)S(1)} %copy-done.2, bf16[6,1024,128]{2,1,0:T(8,128)(2,1)S(1)} %copy-done.7, ...), custom_call_target="tpu_custom_call" | custom-call | flops 17999998976 | bytes 8000000 | tf_op jit(solution)/shard_map/back_0/pallas_call | solution.py:632
  181.7 12.2 %back_1.1 = (bf16[6,1024,128]{2,1,0:T(8,128)(2,1)S(1)}, bf16[4,4,10,48,128]{4,3,2,1,0:T(8,128)(2,1)S(1)}, bf16[4,4,10,48,128]{4,3,2,1,0:T(8,128)(2,1)S(1)}, f32[8,768]{1,0:T(8,128)S(1)}) custom-call(s32[2]{0:T(128)S(1)} %pad_add_fusion.refs_0_, s32[1,2]{1,0:T(1,128)S(1)} %copy-done.2, ...), custom_call_target="tpu_custom_call", output_to_operand_aliasing={{1}: (8, {}), {2}: (9, {})} | custom-call | flops 17999998976 | bytes 8000000 | tf_op jit(solution)/shard_map/back_1/pallas_call | solution.py:632
  195.6 5.1 %collective-permute-done.23 = bf16[2,4,16,48,128]{4,3,2,1,0:T(8,128)(2,1)S(1)} collective-permute-done((bf16[2,4,16,48,128]{4,3,2,1,0:T(8,128)(2,1)S(1)}, bf16[2,4,16,48,128]{4,3,2,1,0:T(8,128)(2,1)S(1)}, u32[]{:S(2)}, u32[]{:S(2)}) %collective-permute-start.23) | collective-permute-done | bytes 1572896 | tf_op jit(solution)/shard_map/ppermute | solution.py:714
  201.0 14.4 %back_2.1 = (bf16[6,1024,128]{2,1,0:T(8,128)(2,1)S(1)}, bf16[4,4,10,48,128]{4,3,2,1,0:T(8,128)(2,1)S(1)}, bf16[4,4,10,48,128]{4,3,2,1,0:T(8,128)(2,1)S(1)}, f32[8,768]{1,0:T(8,128)}) custom-call(s32[2]{0:T(128)S(1)} %pad_add_fusion.refs_0_, s32[1,2]{1,0:T(1,128)S(1)} %copy-done.2, ...), custom_call_target="tpu_custom_call", output_to_operand_aliasing={{1}: (8, {}), {2}: (9, {})} | custom-call | flops 17999998976 | bytes 8000000 | tf_op jit(solution)/shard_map/back_2/pallas_call | solution.py:632
  217.9 4.0 %first_norm_back_0.1.refs_0_ = bf16[1024,768]{1,0:T(8,128)(2,1)} custom-call(bf16[1024,768]{1,0:T(8,128)(2,1)S(1)} %copy-done.1, bf16[6,1024,128]{2,1,0:T(8,128)(2,1)S(1)} %get-tuple-element.96.d_0, bf16[6,1024,128]{2,1,0:T(8,128)(2,1)S(1)} %get-tuple-element.107.d_1, bf16[6,1024,128]{2,1,0:T(8,128)(2,1)S(1)} %get-tuple-element.120.d_2, ...), custom_call_target="tpu_custom_call" | custom-call | flops 8000000000 | bytes 9000000 | tf_op jit(solution)/shard_map/first_norm_back_0/pallas_call | solution.py:680
  221.9 5.7 %collective-permute-done.26 = bf16[4,16,48,128]{3,2,1,0:T(8,128)(2,1)S(1)} collective-permute-done((bf16[4,16,48,128]{3,2,1,0:T(8,128)(2,1)S(1)}, bf16[4,16,48,128]{3,2,1,0:T(8,128)(2,1)S(1)}, u32[]{:S(2)}, u32[]{:S(2)}) %collective-permute-start.26) | collective-permute-done | bytes 786464 | tf_op jit(solution)/shard_map/ppermute | solution.py:714
  229.6 3.6 %collective-permute-start.32 = (bf16[16,48,128]{2,1,0:T(8,128)(2,1)S(1)}, bf16[16,48,128]{2,1,0:T(8,128)(2,1)S(1)}, u32[]{:S(2)}, u32[]{:S(2)}) collective-permute-start(bf16[16,48,128]{2,1,0:T(8,128)(2,1)S(1)} %get-tuple-element.140), channel_id=1, source_target_pairs={{0,24},{1,25},{2,26},{3,27},{4,28},{5,29},{6,30},{7,31},{8,16},{9,... | collective-permute-start | bytes 589832 | tf_op jit(solution)/shard_map/ppermute | solution.py:714
  233.2 3.8 %collective-permute-start.31 = (bf16[16,48,128]{2,1,0:T(8,128)(2,1)S(1)}, bf16[16,48,128]{2,1,0:T(8,128)(2,1)S(1)}, u32[]{:S(2)}, u32[]{:S(2)}) collective-permute-start(bf16[16,48,128]{2,1,0:T(8,128)(2,1)S(1)} %get-tuple-element.141), channel_id=1, source_target_pairs={{0,16},{1,17},{2,18},{3,19},{4,20},{5,21},{6,22},{7,23},{8,24},{9,... | collective-permute-start | bytes 589832 | tf_op jit(solution)/shard_map/ppermute | solution.py:714
  237.0 3.8 %first_norm_back_1.1 = bf16[1024,768]{1,0:T(8,128)(2,1)} custom-call(bf16[1024,768]{1,0:T(8,128)(2,1)S(1)} %copy-done.1, bf16[6,1024,128]{2,1,0:T(8,128)(2,1)S(1)} %get-tuple-element.96.d_0, bf16[6,1024,128]{2,1,0:T(8,128)(2,1)S(1)} %get-tuple-element.107.d_1, bf16[6,1024,128]{2,1,0:T(8,128)(2,1)S(1)} %get-tuple-element.120.d_2, ...), custom_call_target="tpu_custom_call", output_to_operand_aliasing={{}: (9, {})} | custom-call | flops 8000000000 | bytes 9000000 | tf_op jit(solution)/shard_map/first_norm_back_1/pallas_call | solution.py:680
  244.0 5.8 %collective-permute-done.31 = bf16[16,48,128]{2,1,0:T(8,128)(2,1)S(1)} collective-permute-done((bf16[16,48,128]{2,1,0:T(8,128)(2,1)S(1)}, bf16[16,48,128]{2,1,0:T(8,128)(2,1)S(1)}, u32[]{:S(2)}, u32[]{:S(2)}) %collective-permute-start.31) | collective-permute-done | bytes 196640 | tf_op jit(solution)/shard_map/ppermute | solution.py:714
  254.0 6.7 %collective-permute-done.38 = bf16[11,48,128]{2,1,0:T(8,128)(2,1)S(1)} collective-permute-done((bf16[11,48,128]{2,1,0:T(8,128)(2,1)S(1)}, bf16[11,48,128]{2,1,0:T(8,128)(2,1)S(1)}, u32[]{:S(2)}, u32[]{:S(2)}) %collective-permute-start.38) | collective-permute-done | bytes 135200 | tf_op jit(solution)/shard_map/ppermute | solution.py:714
  271.9 5.9 %collective-permute-done.34 = bf16[10,48,128]{2,1,0:T(8,128)(2,1)S(1)} collective-permute-done((bf16[10,48,128]{2,1,0:T(8,128)(2,1)S(1)}, bf16[10,48,128]{2,1,0:T(8,128)(2,1)S(1)}, u32[]{:S(2)}, u32[]{:S(2)}) %collective-permute-start.34) | collective-permute-done | bytes 122912 | tf_op jit(solution)/shard_map/ppermute | solution.py:714
  (218 shorter events, 61.2 us)
Async XLA Ops:
  12.4 15.6 %collective-permute-start.2 = (bf16[27,48,128]{2,1,0:T(8,128)(2,1)S(1)}, bf16[27,48,128]{2,1,0:T(8,128)(2,1)S(1)}, u32[]{:S(2)}, u32[]{:S(2)}) collective-permute-start(bf16[27,48,128]{2,1,0:T(8,128)(2,1)S(1)} %constant_dynamic-update-slice_fusion), channel_id=1, source_target_pairs={{0,8},{1,9},{2,10},{3,11},{4,12},{5,13},{6,14},{7,15},{8,0},{9,1},... | collective-permute-start | bytes 995336 | tf_op jit(solution)/shard_map/ppermute | solution.py:714
  14.2 13.8 %collective-permute-start.6 = (bf16[10,48,128]{2,1,0:T(8,128)(2,1)S(1)}, bf16[10,48,128]{2,1,0:T(8,128)(2,1)S(1)}, u32[]{:S(2)}, u32[]{:S(2)}) collective-permute-start(bf16[10,48,128]{2,1,0:T(8,128)(2,1)S(1)} %constant_dynamic-update-slice_fusion.10), channel_id=1, source_target_pairs={{0,24},{1,25},{2,26},{3,27},{4,28},{5,29},{6,30},{7,31},{8,16},{9,... | collective-permute-start | bytes 368648 | tf_op jit(solution)/shard_map/ppermute | solution.py:714
  16.6 11.3 %collective-permute-start.5 = (bf16[10,48,128]{2,1,0:T(8,128)(2,1)S(1)}, bf16[10,48,128]{2,1,0:T(8,128)(2,1)S(1)}, u32[]{:S(2)}, u32[]{:S(2)}) collective-permute-start(bf16[10,48,128]{2,1,0:T(8,128)(2,1)S(1)} %constant_dynamic-update-slice_fusion.10), channel_id=1, source_target_pairs={{0,16},{1,17},{2,18},{3,19},{4,20},{5,21},{6,22},{7,23},{8,24},{9,... | collective-permute-start | bytes 368648 | tf_op jit(solution)/shard_map/ppermute | solution.py:714
  28.0 17.0 %collective-permute-start.7 = (bf16[4,10,48,128]{3,2,1,0:T(8,128)(2,1)S(1)}, bf16[4,10,48,128]{3,2,1,0:T(8,128)(2,1)}, u32[]{:S(2)}, u32[]{:S(2)}) collective-permute-start(bf16[4,10,48,128]{3,2,1,0:T(8,128)(2,1)S(1)} %pad_maximum_fusion.2.refs_3_.refs_4_), channel_id=1, source_target_pairs={{0,4},{1,3},{2,6},{3,1},{4,0},{5,7},{6,2},{7,5},{8,12},{9,11},{10,... | collective-permute-start | bytes 1474568 | tf_op jit(solution)/shard_map/ppermute | solution.py:714
  29.6 15.4 %collective-permute-start.3 = (bf16[27,48,128]{2,1,0:T(8,128)(2,1)S(1)}, bf16[27,48,128]{2,1,0:T(8,128)(2,1)S(1)}, u32[]{:S(2)}, u32[]{:S(2)}) collective-permute-start(bf16[27,48,128]{2,1,0:T(8,128)(2,1)S(1)} %constant_dynamic-update-slice_fusion), channel_id=1, source_target_pairs={{0,16},{1,17},{2,18},{3,19},{4,20},{5,21},{6,22},{7,23},{8,24},{9,... | collective-permute-start | bytes 995336 | tf_op jit(solution)/shard_map/ppermute | solution.py:714
  31.4 18.1 %collective-permute-start.9 = (bf16[4,10,48,128]{3,2,1,0:T(8,128)(2,1)S(1)}, bf16[4,10,48,128]{3,2,1,0:T(8,128)(2,1)}, u32[]{:S(2)}, u32[]{:S(2)}) collective-permute-start(bf16[4,10,48,128]{3,2,1,0:T(8,128)(2,1)S(1)} %pad_maximum_fusion.2.refs_3_.refs_4_), channel_id=1, source_target_pairs={{0,2},{1,5},{2,0},{3,7},{4,6},{5,1},{6,4},{7,3},{8,10},{9,13},{10,... | collective-permute-start | bytes 1474568 | tf_op jit(solution)/shard_map/ppermute | solution.py:714
  45.6 12.3 %collective-permute-start.4 = (bf16[27,48,128]{2,1,0:T(8,128)(2,1)S(1)}, bf16[27,48,128]{2,1,0:T(8,128)(2,1)S(1)}, u32[]{:S(2)}, u32[]{:S(2)}) collective-permute-start(bf16[27,48,128]{2,1,0:T(8,128)(2,1)S(1)} %constant_dynamic-update-slice_fusion), channel_id=1, source_target_pairs={{0,24},{1,25},{2,26},{3,27},{4,28},{5,29},{6,30},{7,31},{8,16},{9,... | collective-permute-start | bytes 995336 | tf_op jit(solution)/shard_map/ppermute | solution.py:714
  59.0 31.1 %collective-permute-start.14 = (bf16[4,27,48,128]{3,2,1,0:T(8,128)(2,1)S(1)}, bf16[4,27,48,128]{3,2,1,0:T(8,128)(2,1)}, u32[]{:S(2)}, u32[]{:S(2)}) collective-permute-start(bf16[4,27,48,128]{3,2,1,0:T(8,128)(2,1)S(1)} %pad_maximum_fusion.refs_8_), channel_id=1, source_target_pairs={{0,4},{1,3},{2,6},{3,1},{4,0},{5,7},{6,2},{7,5},{8,12},{9,11},{10,... | collective-permute-start | bytes 3981320 | tf_op jit(solution)/shard_map/ppermute | solution.py:714
  59.7 43.2 %collective-permute-start.15 = (bf16[4,27,48,128]{3,2,1,0:T(8,128)(2,1)S(1)}, bf16[4,27,48,128]{3,2,1,0:T(8,128)(2,1)S(1)}, u32[]{:S(2)}, u32[]{:S(2)}) collective-permute-start(bf16[4,27,48,128]{3,2,1,0:T(8,128)(2,1)S(1)} %pad_maximum_fusion.refs_8_), channel_id=1, source_target_pairs={{0,2},{1,5},{2,0},{3,7},{4,6},{5,1},{6,4},{7,3},{8,10},{9,13},{10,... | collective-permute-start | bytes 3981320 | tf_op jit(solution)/shard_map/ppermute | solution.py:714
  90.1 18.0 %collective-permute-start.16 = (bf16[4,27,48,128]{3,2,1,0:T(8,128)(2,1)}, bf16[4,27,48,128]{3,2,1,0:T(8,128)(2,1)S(1)}, u32[]{:S(2)}, u32[]{:S(2)}) collective-permute-start(bf16[4,27,48,128]{3,2,1,0:T(8,128)(2,1)} %collective-permute-done.14.refs_9_), channel_id=1, source_target_pairs={{0,2},{1,5},{2,0},{3,7},{4,6},{5,1},{6,4},{7,3},{8,10},{9,13},{10,... | collective-permute-start | bytes 3981320 | tf_op jit(solution)/shard_map/ppermute | solution.py:714
  91.6 16.6 %collective-permute-start.17 = (bf16[4,27,48,128]{3,2,1,0:T(8,128)(2,1)S(1)}, bf16[4,27,48,128]{3,2,1,0:T(8,128)(2,1)S(1)}, u32[]{:S(2)}, u32[]{:S(2)}) collective-permute-start(bf16[4,27,48,128]{3,2,1,0:T(8,128)(2,1)S(1)} %pad_maximum_fusion.refs_8_), channel_id=1, source_target_pairs={{0,1},{1,0},{2,3},{3,2},{4,5},{5,4},{6,7},{7,6},{8,9},{9,8},{10,11... | collective-permute-start | bytes 3981320 | tf_op jit(solution)/shard_map/ppermute | solution.py:714
  164.6 15.2 %collective-permute-start.21 = (bf16[4,4,16,48,128]{4,3,2,1,0:T(8,128)(2,1)}, bf16[4,4,16,48,128]{4,3,2,1,0:T(8,128)(2,1)S(1)}, u32[]{:S(2)}, u32[]{:S(2)}) collective-permute-start(bf16[4,4,16,48,128]{4,3,2,1,0:T(8,128)(2,1)} %get-tuple-element.99), channel_id=1, source_target_pairs={{0,1},{1,0},{2,3},{3,2},{4,5},{5,4},{6,7},{7,6},{8,9},{9,8},{10,11... | collective-permute-start | bytes 9437192 | tf_op jit(solution)/shard_map/ppermute | solution.py:714
  164.8 16.9 %collective-permute-start.22 = (bf16[4,4,11,48,128]{4,3,2,1,0:T(8,128)(2,1)}, bf16[4,4,11,48,128]{4,3,2,1,0:T(8,128)(2,1)S(1)}, u32[]{:S(2)}, u32[]{:S(2)}) collective-permute-start(bf16[4,4,11,48,128]{4,3,2,1,0:T(8,128)(2,1)} %get-tuple-element.101), channel_id=1, source_target_pairs={{0,1},{1,0},{2,3},{3,2},{4,5},{5,4},{6,7},{7,6},{8,9},{9,8},{10,11... | collective-permute-start | bytes 6488072 | tf_op jit(solution)/shard_map/ppermute | solution.py:714
  180.2 20.5 %collective-permute-start.23 = (bf16[2,4,16,48,128]{4,3,2,1,0:T(8,128)(2,1)S(1)}, bf16[2,4,16,48,128]{4,3,2,1,0:T(8,128)(2,1)S(1)}, u32[]{:S(2)}, u32[]{:S(2)}) collective-permute-start(bf16[2,4,16,48,128]{4,3,2,1,0:T(8,128)(2,1)S(1)} %add_convert_fusion), channel_id=1, source_target_pairs={{0,2},{1,5},{2,0},{3,7},{4,6},{5,1},{6,4},{7,3},{8,10},{9,13},{10,... | collective-permute-start | bytes 4718600 | tf_op jit(solution)/shard_map/ppermute | solution.py:714
  194.2 21.7 %collective-permute-start.24 = (bf16[2,4,11,48,128]{4,3,2,1,0:T(8,128)(2,1)S(1)}, bf16[2,4,11,48,128]{4,3,2,1,0:T(8,128)(2,1)S(1)}, u32[]{:S(2)}, u32[]{:S(2)}) collective-permute-start(bf16[2,4,11,48,128]{4,3,2,1,0:T(8,128)(2,1)S(1)} %add_convert_fusion.1), channel_id=1, source_target_pairs={{0,2},{1,5},{2,0},{3,7},{4,6},{5,1},{6,4},{7,3},{8,10},{9,13},{10,... | collective-permute-start | bytes 3244040 | tf_op jit(solution)/shard_map/ppermute | solution.py:714
  215.4 12.1 %collective-permute-start.25 = (bf16[4,4,10,48,128]{4,3,2,1,0:T(8,128)(2,1)S(1)}, bf16[4,4,10,48,128]{4,3,2,1,0:T(8,128)(2,1)S(1)}, u32[]{:S(2)}, u32[]{:S(2)}) collective-permute-start(bf16[4,4,10,48,128]{4,3,2,1,0:T(8,128)(2,1)S(1)} %get-tuple-element.125), channel_id=1, source_target_pairs={{0,1},{1,0},{2,3},{3,2},{4,5},{5,4},{6,7},{7,6},{8,9},{9,8},{10,11... | collective-permute-start | bytes 5898248 | tf_op jit(solution)/shard_map/ppermute | solution.py:714
  215.5 12.1 %collective-permute-start.26 = (bf16[4,16,48,128]{3,2,1,0:T(8,128)(2,1)S(1)}, bf16[4,16,48,128]{3,2,1,0:T(8,128)(2,1)S(1)}, u32[]{:S(2)}, u32[]{:S(2)}) collective-permute-start(bf16[4,16,48,128]{3,2,1,0:T(8,128)(2,1)S(1)} %fusion), channel_id=1, source_target_pairs={{0,4},{1,3},{2,6},{3,1},{4,0},{5,7},{6,2},{7,5},{8,12},{9,11},{10,... | collective-permute-start | bytes 2359304 | tf_op jit(solution)/shard_map/ppermute | solution.py:714
  216.1 33.9 %collective-permute-start.29 = (bf16[4,11,48,128]{3,2,1,0:T(8,128)(2,1)S(1)}, bf16[4,11,48,128]{3,2,1,0:T(8,128)(2,1)S(1)}, u32[]{:S(2)}, u32[]{:S(2)}) collective-permute-start(bf16[4,11,48,128]{3,2,1,0:T(8,128)(2,1)S(1)} %fusion.1), channel_id=1, source_target_pairs={{0,4},{1,3},{2,6},{3,1},{4,0},{5,7},{6,2},{7,5},{8,12},{9,11},{10,... | collective-permute-start | bytes 1622024 | tf_op jit(solution)/shard_map/ppermute | solution.py:714
  227.8 15.5 %collective-permute-start.27 = (bf16[2,4,10,48,128]{4,3,2,1,0:T(8,128)(2,1)S(1)}, bf16[2,4,10,48,128]{4,3,2,1,0:T(8,128)(2,1)S(1)}, u32[]{:S(2)}, u32[]{:S(2)}) collective-permute-start(bf16[2,4,10,48,128]{4,3,2,1,0:T(8,128)(2,1)S(1)} %add_convert_fusion.2), channel_id=1, source_target_pairs={{0,2},{1,5},{2,0},{3,7},{4,6},{5,1},{6,4},{7,3},{8,10},{9,13},{10,... | collective-permute-start | bytes 2949128 | tf_op jit(solution)/shard_map/ppermute | solution.py:714
  229.6 14.4 %collective-permute-start.32 = (bf16[16,48,128]{2,1,0:T(8,128)(2,1)S(1)}, bf16[16,48,128]{2,1,0:T(8,128)(2,1)S(1)}, u32[]{:S(2)}, u32[]{:S(2)}) collective-permute-start(bf16[16,48,128]{2,1,0:T(8,128)(2,1)S(1)} %get-tuple-element.140), channel_id=1, source_target_pairs={{0,24},{1,25},{2,26},{3,27},{4,28},{5,29},{6,30},{7,31},{8,16},{9,... | collective-permute-start | bytes 589832 | tf_op jit(solution)/shard_map/ppermute | solution.py:714
  233.2 16.6 %collective-permute-start.31 = (bf16[16,48,128]{2,1,0:T(8,128)(2,1)S(1)}, bf16[16,48,128]{2,1,0:T(8,128)(2,1)S(1)}, u32[]{:S(2)}, u32[]{:S(2)}) collective-permute-start(bf16[16,48,128]{2,1,0:T(8,128)(2,1)S(1)} %get-tuple-element.141), channel_id=1, source_target_pairs={{0,16},{1,17},{2,18},{3,19},{4,20},{5,21},{6,22},{7,23},{8,24},{9,... | collective-permute-start | bytes 589832 | tf_op jit(solution)/shard_map/ppermute | solution.py:714
  237.0 12.8 %collective-permute-start.30 = (bf16[16,48,128]{2,1,0:T(8,128)(2,1)S(1)}, bf16[16,48,128]{2,1,0:T(8,128)(2,1)S(1)}, u32[]{:S(2)}, u32[]{:S(2)}) collective-permute-start(bf16[16,48,128]{2,1,0:T(8,128)(2,1)S(1)} %get-tuple-element.142), channel_id=1, source_target_pairs={{0,8},{1,9},{2,10},{3,11},{4,12},{5,13},{6,14},{7,15},{8,0},{9,1},... | collective-permute-start | bytes 589832 | tf_op jit(solution)/shard_map/ppermute | solution.py:714
  250.2 13.0 %collective-permute-start.37 = (bf16[11,48,128]{2,1,0:T(8,128)(2,1)S(1)}, bf16[11,48,128]{2,1,0:T(8,128)(2,1)S(1)}, u32[]{:S(2)}, u32[]{:S(2)}) collective-permute-start(bf16[11,48,128]{2,1,0:T(8,128)(2,1)S(1)} %get-tuple-element.143), channel_id=1, source_target_pairs={{0,16},{1,17},{2,18},{3,19},{4,20},{5,21},{6,22},{7,23},{8,24},{9,... | collective-permute-start | bytes 405512 | tf_op jit(solution)/shard_map/ppermute | solution.py:714
  265.8 12.0 %collective-permute-start.34 = (bf16[10,48,128]{2,1,0:T(8,128)(2,1)S(1)}, bf16[10,48,128]{2,1,0:T(8,128)(2,1)S(1)}, u32[]{:S(2)}, u32[]{:S(2)}) collective-permute-start(bf16[10,48,128]{2,1,0:T(8,128)(2,1)S(1)} %get-tuple-element.147), channel_id=1, source_target_pairs={{0,16},{1,17},{2,18},{3,19},{4,20},{5,21},{6,22},{7,23},{8,24},{9,... | collective-permute-start | bytes 368648 | tf_op jit(solution)/shard_map/ppermute | solution.py:714
  (45 other events, 442.5 us)

commit v2 on v1

--- a/solution.py
+++ b/solution.py
@@ -964,7 +964,7 @@
         total_a = ff_a.end(at.sum_1)
         ff_b.line(total_a)
         at.line(*ff_b.sum_0)
-        g_qkv, g_out, g_up, g_down, vecs = fast_grads(at.end(), total_a, ff_b.end(*at.sum_0))
+        g_qkv, g_out, g_up, g_down, vecs = fast_grads(at.end(), total_a, ff_b.end(at.far[0]))
     else:
         g_qkv, g_out, g_up, g_down, vecs = plain_grads(own, own_a, own_b)
     return (

time: 286 us -> 283 us (0.990)
  waiting for transfers between devices: 86.1 us -> 81.3 us
    ppermute x40, waiting for transfers between devices: 86.1 us -> 81.3 us  [send(): return lax.ppermute(value, BOTH, pairs)]
  transfers between devices with their start and end apart: 40 -> 40, of which waited for: 18 -> 15; matrix products, arithmetic and copies ran while one was open for 2% -> 3% of each run, Pallas kernels for 29% -> 29%
where the time goes in v2:
time: 283 us; the launch traced here: 279 us
  Pallas kernels  134 us (47%)
  waiting for transfers between devices  81.3 us (29%)
  starting transfers between devices  44.9 us (16%)
  other arithmetic  9.79 us (3%)
  local copies, waits for them, and re-layouts  6.83 us (2%)
    ppermute x40, waiting for transfers between devices, send(): return lax.ppermute(value, BOTH, pairs)  81.3 us
    pallas_call x1, Pallas kernels, middle(): pl.pallas_call(lambda *refs: middle_body(pieces, *refs), out_shape=(sds((...  52.3 us
    ppermute x40, starting transfers between devices, send(): return lax.ppermute(value, BOTH, pairs)  44.9 us
    pallas_call x3, Pallas kernels, back(): pl.pallas_call(lambda *refs: back_body(pieces, third, *refs), out_shape=(...  38.3 us
    pallas_call x3, Pallas kernels, front(): pl.pallas_call(lambda *refs: front_body(pieces, third, *refs), out_shape=...  35.8 us
    pallas_call x2, Pallas kernels, first_norm_back(): pl.pallas_call(first_norm_back_body, grid=(1,), out_shape=sds((ROWS, D),...  7.82 us
  transfers between devices with their start and end apart: 40, of which 15 were waited for; matrix products, arithmetic and copies ran while one was open for 3% of the time, Pallas kernels for 29%

profile of v2, /device:TPU:0, one launch (start us, length us, event | category | flops | bytes accessed | tf_op | source)
XLA Modules:
  0.0 278.9 jit_solution(3925947153508061696)
XLA Ops:
  8.5 4.0 %collective-permute-done.1 = bf16[10,48,128]{2,1,0:T(8,128)(2,1)S(1)} collective-permute-done((bf16[10,48,128]{2,1,0:T(8,128)(2,1)S(1)}, bf16[10,48,128]{2,1,0:T(8,128)(2,1)S(1)}, u32[]{:S(2)}, u32[]{:S(2)}) %collective-permute-start.1) | collective-permute-done | bytes 122912 | tf_op jit(solution)/shard_map/ppermute | solution.py:714
  16.7 11.2 %collective-permute-done.6 = bf16[10,48,128]{2,1,0:T(8,128)(2,1)S(1)} collective-permute-done((bf16[10,48,128]{2,1,0:T(8,128)(2,1)S(1)}, bf16[10,48,128]{2,1,0:T(8,128)(2,1)S(1)}, u32[]{:S(2)}, u32[]{:S(2)}) %collective-permute-start.6) | collective-permute-done | bytes 122912 | tf_op jit(solution)/shard_map/ppermute | solution.py:714
  32.9 12.1 %collective-permute-done.3 = bf16[27,48,128]{2,1,0:T(8,128)(2,1)S(1)} collective-permute-done((bf16[27,48,128]{2,1,0:T(8,128)(2,1)S(1)}, bf16[27,48,128]{2,1,0:T(8,128)(2,1)S(1)}, u32[]{:S(2)}, u32[]{:S(2)}) %collective-permute-start.3) | collective-permute-done | bytes 331808 | tf_op jit(solution)/shard_map/ppermute | solution.py:714
  50.1 4.1 %collective-permute-done.8.refs_6_.refs_7_ = bf16[4,10,48,128]{3,2,1,0:T(8,128)(2,1)} collective-permute-done((bf16[4,10,48,128]{3,2,1,0:T(8,128)(2,1)}, bf16[4,10,48,128]{3,2,1,0:T(8,128)(2,1)}, u32[]{:S(2)}, u32[]{:S(2)}) %collective-permute-start.8) | collective-permute-done | bytes 491552 | tf_op jit(solution)/shard_map/ppermute | solution.py:714
  54.2 3.7 %collective-permute-done.4 = bf16[27,48,128]{2,1,0:T(8,128)(2,1)S(1)} collective-permute-done((bf16[27,48,128]{2,1,0:T(8,128)(2,1)S(1)}, bf16[27,48,128]{2,1,0:T(8,128)(2,1)S(1)}, u32[]{:S(2)}, u32[]{:S(2)}) %collective-permute-start.4) | collective-permute-done | bytes 331808 | tf_op jit(solution)/shard_map/ppermute | solution.py:714
  60.3 14.1 %front_0.1 = (bf16[1024,768]{1,0:T(8,128)(2,1)S(1)}, bf16[768,1024]{1,0:T(8,128)(2,1)S(1)}, f32[16,768]{1,0:T(8,128)S(1)}, bf16[6,1024,128]{2,1,0:T(8,128)(2,1)S...) custom-call(s32[2]{0:T(128)S(1)} %pad_add_fusion.refs_0_, ...), custom_call_target="tpu_custom_call" | custom-call | flops 6000000000 | bytes 8000000 | tf_op jit(solution)/shard_map/front_0/pallas_call | solution.py:272
  74.4 11.0 %front_1.1 = (bf16[6,1024,128]{2,1,0:T(8,128)(2,1)S(1)}, bf16[2,1024,128]{2,1,0:T(8,128)(2,1)S(1)}, f32[2,8,1024]{2,1,0:T(8,128)S(1)}, bf16[6,16,48,128]{3,2,1,0:T(8,128)(2,1)S(1)}) custom-call(s32[2]{0:T(128)S(1)} %pad_add_fusion.refs_0_, s32[1,2]{1,0:T(1,128)S(1)} %copy-done.2, bf16[1024,768]{1,0:T(8,128)(2,1)S(1)} %get-tuple-element.82.refs_2_, ...), custom_call_target="tpu_custom_call" | custom-call | flops 6000000000 | bytes 8000000 | tf_op jit(solution)/shard_map/front_1/pallas_call | solution.py:272
  85.3 4.8 %collective-permute-done.14.refs_9_ = bf16[4,27,48,128]{3,2,1,0:T(8,128)(2,1)} collective-permute-done((bf16[4,27,48,128]{3,2,1,0:T(8,128)(2,1)S(1)}, bf16[4,27,48,128]{3,2,1,0:T(8,128)(2,1)}, u32[]{:S(2)}, u32[]{:S(2)}) %collective-permute-start.14) | collective-permute-done | bytes 1327136 | tf_op jit(solution)/shard_map/ppermute | solution.py:714
  91.6 10.8 %front_2.1 = (bf16[6,1024,128]{2,1,0:T(8,128)(2,1)S(1)}, bf16[2,1024,128]{2,1,0:T(8,128)(2,1)S(1)}, f32[2,8,1024]{2,1,0:T(8,128)S(1)}, bf16[6,16,48,128]{3,2,1,0:T(8,128)(2,1)S(1)}) custom-call(s32[2]{0:T(128)S(1)} %pad_add_fusion.refs_0_, s32[1,2]{1,0:T(1,128)S(1)} %copy-done.2, bf16[1024,768]{1,0:T(8,128)(2,1)S(1)} %get-tuple-element.82.refs_2_, ...), custom_call_target="tpu_custom_call" | custom-call | flops 6000000000 | bytes 8000000 | tf_op jit(solution)/shard_map/front_2/pallas_call | solution.py:272
  103.0 5.1 %collective-permute-done.16.refs_11_ = bf16[4,27,48,128]{3,2,1,0:T(8,128)(2,1)S(1)} collective-permute-done((bf16[4,27,48,128]{3,2,1,0:T(8,128)(2,1)}, bf16[4,27,48,128]{3,2,1,0:T(8,128)(2,1)S(1)}, u32[]{:S(2)}, u32[]{:S(2)}) %collective-permute-start.16) | collective-permute-done | bytes 1327136 | tf_op jit(solution)/shard_map/ppermute | solution.py:714
  112.3 52.3 %middle.1 = (bf16[1024,768]{1,0:T(8,128)(2,1)}, f32[1024,768]{1,0:T(8,128)}, bf16[6,1024,128]{2,1,0:T(8,128)(2,1)}, bf16[4,4,16,48,128]{4,3,2,1,0:T(8,128)(2,1)}...) custom-call(s32[2]{0:T(128)S(1)} %pad_add_fusion.refs_0_, ...), custom_call_target="tpu_custom_call" | custom-call | flops 60000002048 | bytes 40000000 | tf_op jit(solution)/shard_map/middle/pallas_call | solution.py:461
  168.0 11.8 %back_0.1 = (bf16[6,1024,128]{2,1,0:T(8,128)(2,1)S(1)}, bf16[4,4,10,48,128]{4,3,2,1,0:T(8,128)(2,1)S(1)}, bf16[4,4,10,48,128]{4,3,2,1,0:T(8,128)(2,1)S(1)}, f32[8,768]{1,0:T(8,128)S(1)}) custom-call(s32[2]{0:T(128)S(1)} %pad_add_fusion.refs_0_, s32[1,2]{1,0:T(1,128)S(1)} %copy-done.2, bf16[6,1024,128]{2,1,0:T(8,128)(2,1)S(1)} %copy-done.7, ...), custom_call_target="tpu_custom_call" | custom-call | flops 17999998976 | bytes 8000000 | tf_op jit(solution)/shard_map/back_0/pallas_call | solution.py:632
  181.7 12.2 %back_1.1 = (bf16[6,1024,128]{2,1,0:T(8,128)(2,1)S(1)}, bf16[4,4,10,48,128]{4,3,2,1,0:T(8,128)(2,1)S(1)}, bf16[4,4,10,48,128]{4,3,2,1,0:T(8,128)(2,1)S(1)}, f32[8,768]{1,0:T(8,128)S(1)}) custom-call(s32[2]{0:T(128)S(1)} %pad_add_fusion.refs_0_, s32[1,2]{1,0:T(1,128)S(1)} %copy-done.2, ...), custom_call_target="tpu_custom_call", output_to_operand_aliasing={{1}: (8, {}), {2}: (9, {})} | custom-call | flops 17999998976 | bytes 8000000 | tf_op jit(solution)/shard_map/back_1/pallas_call | solution.py:632
  195.6 5.1 %collective-permute-done.23 = bf16[2,4,16,48,128]{4,3,2,1,0:T(8,128)(2,1)S(1)} collective-permute-done((bf16[2,4,16,48,128]{4,3,2,1,0:T(8,128)(2,1)S(1)}, bf16[2,4,16,48,128]{4,3,2,1,0:T(8,128)(2,1)S(1)}, u32[]{:S(2)}, u32[]{:S(2)}) %collective-permute-start.23) | collective-permute-done | bytes 1572896 | tf_op jit(solution)/shard_map/ppermute | solution.py:714
  201.0 14.4 %back_2.1 = (bf16[6,1024,128]{2,1,0:T(8,128)(2,1)S(1)}, bf16[4,4,10,48,128]{4,3,2,1,0:T(8,128)(2,1)S(1)}, bf16[4,4,10,48,128]{4,3,2,1,0:T(8,128)(2,1)S(1)}, f32[8,768]{1,0:T(8,128)}) custom-call(s32[2]{0:T(128)S(1)} %pad_add_fusion.refs_0_, s32[1,2]{1,0:T(1,128)S(1)} %copy-done.2, ...), custom_call_target="tpu_custom_call", output_to_operand_aliasing={{1}: (8, {}), {2}: (9, {})} | custom-call | flops 17999998976 | bytes 8000000 | tf_op jit(solution)/shard_map/back_2/pallas_call | solution.py:632
  217.9 4.0 %first_norm_back_0.1.refs_0_ = bf16[1024,768]{1,0:T(8,128)(2,1)} custom-call(bf16[1024,768]{1,0:T(8,128)(2,1)S(1)} %copy-done.1, bf16[6,1024,128]{2,1,0:T(8,128)(2,1)S(1)} %get-tuple-element.96.d_0, bf16[6,1024,128]{2,1,0:T(8,128)(2,1)S(1)} %get-tuple-element.107.d_1, bf16[6,1024,128]{2,1,0:T(8,128)(2,1)S(1)} %get-tuple-element.120.d_2, ...), custom_call_target="tpu_custom_call" | custom-call | flops 8000000000 | bytes 9000000 | tf_op jit(solution)/shard_map/first_norm_back_0/pallas_call | solution.py:680
  221.9 5.7 %collective-permute-done.26 = bf16[4,16,48,128]{3,2,1,0:T(8,128)(2,1)S(1)} collective-permute-done((bf16[4,16,48,128]{3,2,1,0:T(8,128)(2,1)S(1)}, bf16[4,16,48,128]{3,2,1,0:T(8,128)(2,1)S(1)}, u32[]{:S(2)}, u32[]{:S(2)}) %collective-permute-start.26) | collective-permute-done | bytes 786464 | tf_op jit(solution)/shard_map/ppermute | solution.py:714
  229.6 3.6 %collective-permute-start.32 = (bf16[16,48,128]{2,1,0:T(8,128)(2,1)S(1)}, bf16[16,48,128]{2,1,0:T(8,128)(2,1)S(1)}, u32[]{:S(2)}, u32[]{:S(2)}) collective-permute-start(bf16[16,48,128]{2,1,0:T(8,128)(2,1)S(1)} %get-tuple-element.140), channel_id=1, source_target_pairs={{0,24},{1,25},{2,26},{3,27},{4,28},{5,29},{6,30},{7,31},{8,16},{9,... | collective-permute-start | bytes 589832 | tf_op jit(solution)/shard_map/ppermute | solution.py:714
  233.2 3.8 %collective-permute-start.31 = (bf16[16,48,128]{2,1,0:T(8,128)(2,1)S(1)}, bf16[16,48,128]{2,1,0:T(8,128)(2,1)S(1)}, u32[]{:S(2)}, u32[]{:S(2)}) collective-permute-start(bf16[16,48,128]{2,1,0:T(8,128)(2,1)S(1)} %get-tuple-element.141), channel_id=1, source_target_pairs={{0,16},{1,17},{2,18},{3,19},{4,20},{5,21},{6,22},{7,23},{8,24},{9,... | collective-permute-start | bytes 589832 | tf_op jit(solution)/shard_map/ppermute | solution.py:714
  237.0 3.8 %first_norm_back_1.1 = bf16[1024,768]{1,0:T(8,128)(2,1)} custom-call(bf16[1024,768]{1,0:T(8,128)(2,1)S(1)} %copy-done.1, bf16[6,1024,128]{2,1,0:T(8,128)(2,1)S(1)} %get-tuple-element.96.d_0, bf16[6,1024,128]{2,1,0:T(8,128)(2,1)S(1)} %get-tuple-element.107.d_1, bf16[6,1024,128]{2,1,0:T(8,128)(2,1)S(1)} %get-tuple-element.120.d_2, ...), custom_call_target="tpu_custom_call", output_to_operand_aliasing={{}: (9, {})} | custom-call | flops 8000000000 | bytes 9000000 | tf_op jit(solution)/shard_map/first_norm_back_1/pallas_call | solution.py:680
  244.0 5.8 %collective-permute-done.31 = bf16[16,48,128]{2,1,0:T(8,128)(2,1)S(1)} collective-permute-done((bf16[16,48,128]{2,1,0:T(8,128)(2,1)S(1)}, bf16[16,48,128]{2,1,0:T(8,128)(2,1)S(1)}, u32[]{:S(2)}, u32[]{:S(2)}) %collective-permute-start.31) | collective-permute-done | bytes 196640 | tf_op jit(solution)/shard_map/ppermute | solution.py:714
  254.0 4.7 %collective-permute-start.33 = (bf16[10,48,128]{2,1,0:T(8,128)(2,1)S(1)}, bf16[10,48,128]{2,1,0:T(8,128)(2,1)S(1)}, u32[]{:S(2)}, u32[]{:S(2)}) collective-permute-start(bf16[10,48,128]{2,1,0:T(8,128)(2,1)S(1)} %get-tuple-element.148), channel_id=1, source_target_pairs={{0,8},{1,9},{2,10},{3,11},{4,12},{5,13},{6,14},{7,15},{8,0},{9,1},... | collective-permute-start | bytes 368648 | tf_op jit(solution)/shard_map/ppermute | solution.py:714
  261.7 5.4 %collective-permute-done.33 = bf16[10,48,128]{2,1,0:T(8,128)(2,1)S(1)} collective-permute-done((bf16[10,48,128]{2,1,0:T(8,128)(2,1)S(1)}, bf16[10,48,128]{2,1,0:T(8,128)(2,1)S(1)}, u32[]{:S(2)}, u32[]{:S(2)}) %collective-permute-start.33) | collective-permute-done | bytes 122912 | tf_op jit(solution)/shard_map/ppermute | solution.py:714
  267.2 6.8 %collective-permute-done.34 = bf16[10,48,128]{2,1,0:T(8,128)(2,1)S(1)} collective-permute-done((bf16[10,48,128]{2,1,0:T(8,128)(2,1)S(1)}, bf16[10,48,128]{2,1,0:T(8,128)(2,1)S(1)}, u32[]{:S(2)}, u32[]{:S(2)}) %collective-permute-start.34) | collective-permute-done | bytes 122912 | tf_op jit(solution)/shard_map/ppermute | solution.py:714
  (218 shorter events, 56.9 us)
Async XLA Ops:
  12.4 15.6 %collective-permute-start.2 = (bf16[27,48,128]{2,1,0:T(8,128)(2,1)S(1)}, bf16[27,48,128]{2,1,0:T(8,128)(2,1)S(1)}, u32[]{:S(2)}, u32[]{:S(2)}) collective-permute-start(bf16[27,48,128]{2,1,0:T(8,128)(2,1)S(1)} %constant_dynamic-update-slice_fusion), channel_id=1, source_target_pairs={{0,8},{1,9},{2,10},{3,11},{4,12},{5,13},{6,14},{7,15},{8,0},{9,1},... | collective-permute-start | bytes 995336 | tf_op jit(solution)/shard_map/ppermute | solution.py:714
  14.2 13.8 %collective-permute-start.6 = (bf16[10,48,128]{2,1,0:T(8,128)(2,1)S(1)}, bf16[10,48,128]{2,1,0:T(8,128)(2,1)S(1)}, u32[]{:S(2)}, u32[]{:S(2)}) collective-permute-start(bf16[10,48,128]{2,1,0:T(8,128)(2,1)S(1)} %constant_dynamic-update-slice_fusion.10), channel_id=1, source_target_pairs={{0,24},{1,25},{2,26},{3,27},{4,28},{5,29},{6,30},{7,31},{8,16},{9,... | collective-permute-start | bytes 368648 | tf_op jit(solution)/shard_map/ppermute | solution.py:714
  28.0 17.0 %collective-permute-start.7 = (bf16[4,10,48,128]{3,2,1,0:T(8,128)(2,1)S(1)}, bf16[4,10,48,128]{3,2,1,0:T(8,128)(2,1)}, u32[]{:S(2)}, u32[]{:S(2)}) collective-permute-start(bf16[4,10,48,128]{3,2,1,0:T(8,128)(2,1)S(1)} %pad_maximum_fusion.2.refs_3_.refs_4_), channel_id=1, source_target_pairs={{0,4},{1,3},{2,6},{3,1},{4,0},{5,7},{6,2},{7,5},{8,12},{9,11},{10,... | collective-permute-start | bytes 1474568 | tf_op jit(solution)/shard_map/ppermute | solution.py:714
  29.6 15.4 %collective-permute-start.3 = (bf16[27,48,128]{2,1,0:T(8,128)(2,1)S(1)}, bf16[27,48,128]{2,1,0:T(8,128)(2,1)S(1)}, u32[]{:S(2)}, u32[]{:S(2)}) collective-permute-start(bf16[27,48,128]{2,1,0:T(8,128)(2,1)S(1)} %constant_dynamic-update-slice_fusion), channel_id=1, source_target_pairs={{0,16},{1,17},{2,18},{3,19},{4,20},{5,21},{6,22},{7,23},{8,24},{9,... | collective-permute-start | bytes 995336 | tf_op jit(solution)/shard_map/ppermute | solution.py:714
  31.4 18.1 %collective-permute-start.9 = (bf16[4,10,48,128]{3,2,1,0:T(8,128)(2,1)S(1)}, bf16[4,10,48,128]{3,2,1,0:T(8,128)(2,1)}, u32[]{:S(2)}, u32[]{:S(2)}) collective-permute-start(bf16[4,10,48,128]{3,2,1,0:T(8,128)(2,1)S(1)} %pad_maximum_fusion.2.refs_3_.refs_4_), channel_id=1, source_target_pairs={{0,2},{1,5},{2,0},{3,7},{4,6},{5,1},{6,4},{7,3},{8,10},{9,13},{10,... | collective-permute-start | bytes 1474568 | tf_op jit(solution)/shard_map/ppermute | solution.py:714
  45.6 12.3 %collective-permute-start.4 = (bf16[27,48,128]{2,1,0:T(8,128)(2,1)S(1)}, bf16[27,48,128]{2,1,0:T(8,128)(2,1)S(1)}, u32[]{:S(2)}, u32[]{:S(2)}) collective-permute-start(bf16[27,48,128]{2,1,0:T(8,128)(2,1)S(1)} %constant_dynamic-update-slice_fusion), channel_id=1, source_target_pairs={{0,24},{1,25},{2,26},{3,27},{4,28},{5,29},{6,30},{7,31},{8,16},{9,... | collective-permute-start | bytes 995336 | tf_op jit(solution)/shard_map/ppermute | solution.py:714
  59.0 31.1 %collective-permute-start.14 = (bf16[4,27,48,128]{3,2,1,0:T(8,128)(2,1)S(1)}, bf16[4,27,48,128]{3,2,1,0:T(8,128)(2,1)}, u32[]{:S(2)}, u32[]{:S(2)}) collective-permute-start(bf16[4,27,48,128]{3,2,1,0:T(8,128)(2,1)S(1)} %pad_maximum_fusion.refs_8_), channel_id=1, source_target_pairs={{0,4},{1,3},{2,6},{3,1},{4,0},{5,7},{6,2},{7,5},{8,12},{9,11},{10,... | collective-permute-start | bytes 3981320 | tf_op jit(solution)/shard_map/ppermute | solution.py:714
  59.7 43.2 %collective-permute-start.15 = (bf16[4,27,48,128]{3,2,1,0:T(8,128)(2,1)S(1)}, bf16[4,27,48,128]{3,2,1,0:T(8,128)(2,1)S(1)}, u32[]{:S(2)}, u32[]{:S(2)}) collective-permute-start(bf16[4,27,48,128]{3,2,1,0:T(8,128)(2,1)S(1)} %pad_maximum_fusion.refs_8_), channel_id=1, source_target_pairs={{0,2},{1,5},{2,0},{3,7},{4,6},{5,1},{6,4},{7,3},{8,10},{9,13},{10,... | collective-permute-start | bytes 3981320 | tf_op jit(solution)/shard_map/ppermute | solution.py:714
  90.1 18.0 %collective-permute-start.16 = (bf16[4,27,48,128]{3,2,1,0:T(8,128)(2,1)}, bf16[4,27,48,128]{3,2,1,0:T(8,128)(2,1)S(1)}, u32[]{:S(2)}, u32[]{:S(2)}) collective-permute-start(bf16[4,27,48,128]{3,2,1,0:T(8,128)(2,1)} %collective-permute-done.14.refs_9_), channel_id=1, source_target_pairs={{0,2},{1,5},{2,0},{3,7},{4,6},{5,1},{6,4},{7,3},{8,10},{9,13},{10,... | collective-permute-start | bytes 3981320 | tf_op jit(solution)/shard_map/ppermute | solution.py:714
  91.6 16.6 %collective-permute-start.17 = (bf16[4,27,48,128]{3,2,1,0:T(8,128)(2,1)S(1)}, bf16[4,27,48,128]{3,2,1,0:T(8,128)(2,1)S(1)}, u32[]{:S(2)}, u32[]{:S(2)}) collective-permute-start(bf16[4,27,48,128]{3,2,1,0:T(8,128)(2,1)S(1)} %pad_maximum_fusion.refs_8_), channel_id=1, source_target_pairs={{0,1},{1,0},{2,3},{3,2},{4,5},{5,4},{6,7},{7,6},{8,9},{9,8},{10,11... | collective-permute-start | bytes 3981320 | tf_op jit(solution)/shard_map/ppermute | solution.py:714
  164.6 15.2 %collective-permute-start.21 = (bf16[4,4,16,48,128]{4,3,2,1,0:T(8,128)(2,1)}, bf16[4,4,16,48,128]{4,3,2,1,0:T(8,128)(2,1)S(1)}, u32[]{:S(2)}, u32[]{:S(2)}) collective-permute-start(bf16[4,4,16,48,128]{4,3,2,1,0:T(8,128)(2,1)} %get-tuple-element.99), channel_id=1, source_target_pairs={{0,1},{1,0},{2,3},{3,2},{4,5},{5,4},{6,7},{7,6},{8,9},{9,8},{10,11... | collective-permute-start | bytes 9437192 | tf_op jit(solution)/shard_map/ppermute | solution.py:714
  164.8 16.9 %collective-permute-start.22 = (bf16[4,4,11,48,128]{4,3,2,1,0:T(8,128)(2,1)}, bf16[4,4,11,48,128]{4,3,2,1,0:T(8,128)(2,1)S(1)}, u32[]{:S(2)}, u32[]{:S(2)}) collective-permute-start(bf16[4,4,11,48,128]{4,3,2,1,0:T(8,128)(2,1)} %get-tuple-element.101), channel_id=1, source_target_pairs={{0,1},{1,0},{2,3},{3,2},{4,5},{5,4},{6,7},{7,6},{8,9},{9,8},{10,11... | collective-permute-start | bytes 6488072 | tf_op jit(solution)/shard_map/ppermute | solution.py:714
  180.2 20.5 %collective-permute-start.23 = (bf16[2,4,16,48,128]{4,3,2,1,0:T(8,128)(2,1)S(1)}, bf16[2,4,16,48,128]{4,3,2,1,0:T(8,128)(2,1)S(1)}, u32[]{:S(2)}, u32[]{:S(2)}) collective-permute-start(bf16[2,4,16,48,128]{4,3,2,1,0:T(8,128)(2,1)S(1)} %add_convert_fusion), channel_id=1, source_target_pairs={{0,2},{1,5},{2,0},{3,7},{4,6},{5,1},{6,4},{7,3},{8,10},{9,13},{10,... | collective-permute-start | bytes 4718600 | tf_op jit(solution)/shard_map/ppermute | solution.py:714
  194.2 21.7 %collective-permute-start.24 = (bf16[2,4,11,48,128]{4,3,2,1,0:T(8,128)(2,1)S(1)}, bf16[2,4,11,48,128]{4,3,2,1,0:T(8,128)(2,1)S(1)}, u32[]{:S(2)}, u32[]{:S(2)}) collective-permute-start(bf16[2,4,11,48,128]{4,3,2,1,0:T(8,128)(2,1)S(1)} %add_convert_fusion.1), channel_id=1, source_target_pairs={{0,2},{1,5},{2,0},{3,7},{4,6},{5,1},{6,4},{7,3},{8,10},{9,13},{10,... | collective-permute-start | bytes 3244040 | tf_op jit(solution)/shard_map/ppermute | solution.py:714
  216.1 33.9 %collective-permute-start.29 = (bf16[4,11,48,128]{3,2,1,0:T(8,128)(2,1)S(1)}, bf16[4,11,48,128]{3,2,1,0:T(8,128)(2,1)S(1)}, u32[]{:S(2)}, u32[]{:S(2)}) collective-permute-start(bf16[4,11,48,128]{3,2,1,0:T(8,128)(2,1)S(1)} %fusion.1), channel_id=1, source_target_pairs={{0,4},{1,3},{2,6},{3,1},{4,0},{5,7},{6,2},{7,5},{8,12},{9,11},{10,... | collective-permute-start | bytes 1622024 | tf_op jit(solution)/shard_map/ppermute | solution.py:714
  227.8 15.5 %collective-permute-start.27 = (bf16[2,4,10,48,128]{4,3,2,1,0:T(8,128)(2,1)S(1)}, bf16[2,4,10,48,128]{4,3,2,1,0:T(8,128)(2,1)S(1)}, u32[]{:S(2)}, u32[]{:S(2)}) collective-permute-start(bf16[2,4,10,48,128]{4,3,2,1,0:T(8,128)(2,1)S(1)} %add_convert_fusion.2), channel_id=1, source_target_pairs={{0,2},{1,5},{2,0},{3,7},{4,6},{5,1},{6,4},{7,3},{8,10},{9,13},{10,... | collective-permute-start | bytes 2949128 | tf_op jit(solution)/shard_map/ppermute | solution.py:714
  229.6 14.4 %collective-permute-start.32 = (bf16[16,48,128]{2,1,0:T(8,128)(2,1)S(1)}, bf16[16,48,128]{2,1,0:T(8,128)(2,1)S(1)}, u32[]{:S(2)}, u32[]{:S(2)}) collective-permute-start(bf16[16,48,128]{2,1,0:T(8,128)(2,1)S(1)} %get-tuple-element.140), channel_id=1, source_target_pairs={{0,24},{1,25},{2,26},{3,27},{4,28},{5,29},{6,30},{7,31},{8,16},{9,... | collective-permute-start | bytes 589832 | tf_op jit(solution)/shard_map/ppermute | solution.py:714
  233.2 16.6 %collective-permute-start.31 = (bf16[16,48,128]{2,1,0:T(8,128)(2,1)S(1)}, bf16[16,48,128]{2,1,0:T(8,128)(2,1)S(1)}, u32[]{:S(2)}, u32[]{:S(2)}) collective-permute-start(bf16[16,48,128]{2,1,0:T(8,128)(2,1)S(1)} %get-tuple-element.141), channel_id=1, source_target_pairs={{0,16},{1,17},{2,18},{3,19},{4,20},{5,21},{6,22},{7,23},{8,24},{9,... | collective-permute-start | bytes 589832 | tf_op jit(solution)/shard_map/ppermute | solution.py:714
  237.0 12.8 %collective-permute-start.30 = (bf16[16,48,128]{2,1,0:T(8,128)(2,1)S(1)}, bf16[16,48,128]{2,1,0:T(8,128)(2,1)S(1)}, u32[]{:S(2)}, u32[]{:S(2)}) collective-permute-start(bf16[16,48,128]{2,1,0:T(8,128)(2,1)S(1)} %get-tuple-element.142), channel_id=1, source_target_pairs={{0,8},{1,9},{2,10},{3,11},{4,12},{5,13},{6,14},{7,15},{8,0},{9,1},... | collective-permute-start | bytes 589832 | tf_op jit(solution)/shard_map/ppermute | solution.py:714
  250.2 16.9 %collective-permute-start.37 = (bf16[11,48,128]{2,1,0:T(8,128)(2,1)S(1)}, bf16[11,48,128]{2,1,0:T(8,128)(2,1)S(1)}, u32[]{:S(2)}, u32[]{:S(2)}) collective-permute-start(bf16[11,48,128]{2,1,0:T(8,128)(2,1)S(1)} %get-tuple-element.143), channel_id=1, source_target_pairs={{0,16},{1,17},{2,18},{3,19},{4,20},{5,21},{6,22},{7,23},{8,24},{9,... | collective-permute-start | bytes 405512 | tf_op jit(solution)/shard_map/ppermute | solution.py:714
  253.3 13.8 %collective-permute-start.36 = (bf16[11,48,128]{2,1,0:T(8,128)(2,1)S(1)}, bf16[11,48,128]{2,1,0:T(8,128)(2,1)S(1)}, u32[]{:S(2)}, u32[]{:S(2)}) collective-permute-start(bf16[11,48,128]{2,1,0:T(8,128)(2,1)S(1)} %get-tuple-element.145), channel_id=1, source_target_pairs={{0,8},{1,9},{2,10},{3,11},{4,12},{5,13},{6,14},{7,15},{8,0},{9,1},... | collective-permute-start | bytes 405512 | tf_op jit(solution)/shard_map/ppermute | solution.py:714
  254.0 13.1 %collective-permute-start.33 = (bf16[10,48,128]{2,1,0:T(8,128)(2,1)S(1)}, bf16[10,48,128]{2,1,0:T(8,128)(2,1)S(1)}, u32[]{:S(2)}, u32[]{:S(2)}) collective-permute-start(bf16[10,48,128]{2,1,0:T(8,128)(2,1)S(1)} %get-tuple-element.148), channel_id=1, source_target_pairs={{0,8},{1,9},{2,10},{3,11},{4,12},{5,13},{6,14},{7,15},{8,0},{9,1},... | collective-permute-start | bytes 368648 | tf_op jit(solution)/shard_map/ppermute | solution.py:714
  258.7 15.3 %collective-permute-start.34 = (bf16[10,48,128]{2,1,0:T(8,128)(2,1)S(1)}, bf16[10,48,128]{2,1,0:T(8,128)(2,1)S(1)}, u32[]{:S(2)}, u32[]{:S(2)}) collective-permute-start(bf16[10,48,128]{2,1,0:T(8,128)(2,1)S(1)} %get-tuple-element.146), channel_id=1, source_target_pairs={{0,16},{1,17},{2,18},{3,19},{4,20},{5,21},{6,22},{7,23},{8,24},{9,... | collective-permute-start | bytes 368648 | tf_op jit(solution)/shard_map/ppermute | solution.py:714
  260.7 13.4 %collective-permute-start.35 = (bf16[10,48,128]{2,1,0:T(8,128)(2,1)S(1)}, bf16[10,48,128]{2,1,0:T(8,128)(2,1)S(1)}, u32[]{:S(2)}, u32[]{:S(2)}) collective-permute-start(bf16[10,48,128]{2,1,0:T(8,128)(2,1)S(1)} %get-tuple-element.147), channel_id=1, source_target_pairs={{0,24},{1,25},{2,26},{3,27},{4,28},{5,29},{6,30},{7,31},{8,16},{9,... | collective-permute-start | bytes 368648 | tf_op jit(solution)/shard_map/ppermute | solution.py:714
  (45 other events, 441.3 us)

commit v3 on v2

--- a/solution.py
+++ b/solution.py
@@ -342,7 +342,8 @@
         dm_s[at, :] = dm
         sums_o[ROW_DN : ROW_DN + 1, :D] += jnp.sum(dm.astype(f32), axis=0, keepdims=True)
 
-    over_rows(prologue)
+    for r in range(ROWS // QB):
+        prologue(pl.ds(QB * r, QB), r)
     a2t_s[...] = a2_s[...].T
     dmt_s[...] = dm_s[...].T
     m_s[...] = jnp.zeros_like(m_s)
@@ -440,7 +441,8 @@
         for g in range(6):
             do_o[g, at, :] = do[:, 128 * g : 128 * g + 128]
 
-    over_rows(epilogue)
+    for r in range(ROWS // QB):
+        epilogue(pl.ds(QB * r, QB), r)
     a2t_s[...] = attended(pl.ds(0, ROWS)).T
     grad = nn(a2t_s[...], dm_s[...])
     for g in range(6):
@@ -491,7 +493,7 @@
             pltpu.SemaphoreType.DMA(()),
         ],
         name="middle",
-        **params(60e9, 40e6, 50),
+        **params(60e9, 40e6, 56),
     )(meta, lens, tokens, *attended, cotangent, vec, *weights)
 
 

time: 283 us -> 284 us (level)
    unnamed x86 -> x108, local copies, waits for them, and re-layouts: 4.25 us -> 7.05 us
  transfers between devices with their start and end apart: 40 -> 40, of which waited for: 15 -> 16; matrix products, arithmetic and copies ran while one was open for 3% -> 3% of each run, Pallas kernels for 29% -> 29%
where the time goes in v3:
time: 284 us; the launch traced here: 281 us
  Pallas kernels  135 us (48%)
  waiting for transfers between devices  78.8 us (28%)
  starting transfers between devices  44.7 us (16%)
  other arithmetic  10.9 us (4%)
  local copies, waits for them, and re-layouts  9.63 us (3%)
    ppermute x40, waiting for transfers between devices, send(): return lax.ppermute(value, BOTH, pairs)  78.8 us
    pallas_call x1, Pallas kernels, middle(): pl.pallas_call(lambda *refs: middle_body(pieces, *refs), out_shape=(sds((...  52.2 us
    ppermute x40, starting transfers between devices, send(): return lax.ppermute(value, BOTH, pairs)  44.7 us
    pallas_call x3, Pallas kernels, back(): pl.pallas_call(lambda *refs: back_body(pieces, third, *refs), out_shape=(...  38.5 us
    pallas_call x3, Pallas kernels, front(): pl.pallas_call(lambda *refs: front_body(pieces, third, *refs), out_shape=...  36.4 us
    pallas_call x2, Pallas kernels, first_norm_back(): pl.pallas_call(first_norm_back_body, grid=(1,), out_shape=sds((ROWS, D),...  7.59 us
    unnamed x108, local copies, waits for them, and re-layouts  7.05 us
  transfers between devices with their start and end apart: 40, of which 16 were waited for; matrix products, arithmetic and copies ran while one was open for 3% of the time, Pallas kernels for 29%

profile of v3, /device:TPU:0, one launch (start us, length us, event | category | flops | bytes accessed | tf_op | source)
XLA Modules:
  0.0 280.5 jit_solution(3326153158068576318)
XLA Ops:
  8.5 4.0 %collective-permute-done.1 = bf16[10,48,128]{2,1,0:T(8,128)(2,1)S(1)} collective-permute-done((bf16[10,48,128]{2,1,0:T(8,128)(2,1)S(1)}, bf16[10,48,128]{2,1,0:T(8,128)(2,1)S(1)}, u32[]{:S(2)}, u32[]{:S(2)}) %collective-permute-start.1) | collective-permute-done | bytes 122912 | tf_op jit(solution)/shard_map/ppermute | solution.py:716
  16.8 11.2 %collective-permute-done.6 = bf16[10,48,128]{2,1,0:T(8,128)(2,1)S(1)} collective-permute-done((bf16[10,48,128]{2,1,0:T(8,128)(2,1)S(1)}, bf16[10,48,128]{2,1,0:T(8,128)(2,1)S(1)}, u32[]{:S(2)}, u32[]{:S(2)}) %collective-permute-start.6) | collective-permute-done | bytes 122912 | tf_op jit(solution)/shard_map/ppermute | solution.py:716
  32.9 12.1 %collective-permute-done.3 = bf16[27,48,128]{2,1,0:T(8,128)(2,1)S(1)} collective-permute-done((bf16[27,48,128]{2,1,0:T(8,128)(2,1)S(1)}, bf16[27,48,128]{2,1,0:T(8,128)(2,1)S(1)}, u32[]{:S(2)}, u32[]{:S(2)}) %collective-permute-start.3) | collective-permute-done | bytes 331808 | tf_op jit(solution)/shard_map/ppermute | solution.py:716
  45.6 3.5 %collective-permute-start.4 = (bf16[27,48,128]{2,1,0:T(8,128)(2,1)}, bf16[27,48,128]{2,1,0:T(8,128)(2,1)S(1)}, u32[]{:S(2)}, u32[]{:S(2)}) collective-permute-start(bf16[27,48,128]{2,1,0:T(8,128)(2,1)} %copy-done.23), channel_id=1, source_target_pairs={{0,24},{1,25},{2,26},{3,27},{4,28},{5,29},{6,30},{7,31},{8,16},{9,... | collective-permute-start | bytes 995336 | tf_op jit(solution)/shard_map/ppermute | solution.py:716
  50.1 3.8 %collective-permute-done.8.refs_6_.refs_7_ = bf16[4,10,48,128]{3,2,1,0:T(8,128)(2,1)S(1)} collective-permute-done((bf16[4,10,48,128]{3,2,1,0:T(8,128)(2,1)S(1)}, bf16[4,10,48,128]{3,2,1,0:T(8,128)(2,1)S(1)}, u32[]{:S(2)}, u32[]{:S(2)}) %collective-permute-start.8) | collective-permute-done | bytes 491552 | tf_op jit(solution)/shard_map/ppermute | solution.py:716
  53.9 4.2 %collective-permute-done.4 = bf16[27,48,128]{2,1,0:T(8,128)(2,1)S(1)} collective-permute-done((bf16[27,48,128]{2,1,0:T(8,128)(2,1)}, bf16[27,48,128]{2,1,0:T(8,128)(2,1)S(1)}, u32[]{:S(2)}, u32[]{:S(2)}) %collective-permute-start.4) | collective-permute-done | bytes 331808 | tf_op jit(solution)/shard_map/ppermute | solution.py:716
  61.5 14.5 %front_0.1 = (bf16[1024,768]{1,0:T(8,128)(2,1)S(1)}, bf16[768,1024]{1,0:T(8,128)(2,1)S(1)}, f32[16,768]{1,0:T(8,128)S(1)}, bf16[6,1024,128]{2,1,0:T(8,128)(2,1)S...) custom-call(s32[2]{0:T(128)S(1)} %pad_add_fusion.refs_0_, ...), custom_call_target="tpu_custom_call" | custom-call | flops 6000000000 | bytes 8000000 | tf_op jit(solution)/shard_map/front_0/pallas_call | solution.py:272
  77.1 10.9 %front_1.1 = (bf16[6,1024,128]{2,1,0:T(8,128)(2,1)S(1)}, bf16[2,1024,128]{2,1,0:T(8,128)(2,1)S(1)}, f32[2,8,1024]{2,1,0:T(8,128)S(1)}, bf16[6,16,48,128]{3,2,1,0:T(8,128)(2,1)S(1)}) custom-call(s32[2]{0:T(128)S(1)} %pad_add_fusion.refs_0_, s32[1,2]{1,0:T(1,128)S(1)} %copy-done.2, bf16[1024,768]{1,0:T(8,128)(2,1)S(1)} %get-tuple-element.82.refs_2_, ...), custom_call_target="tpu_custom_call" | custom-call | flops 6000000000 | bytes 8000000 | tf_op jit(solution)/shard_map/front_1/pallas_call | solution.py:272
  93.0 11.0 %front_2.1 = (bf16[6,1024,128]{2,1,0:T(8,128)(2,1)S(1)}, bf16[2,1024,128]{2,1,0:T(8,128)(2,1)S(1)}, f32[2,8,1024]{2,1,0:T(8,128)S(1)}, bf16[6,16,48,128]{3,2,1,0:T(8,128)(2,1)S(1)}) custom-call(s32[2]{0:T(128)S(1)} %pad_add_fusion.refs_0_, s32[1,2]{1,0:T(1,128)S(1)} %copy-done.2, bf16[1024,768]{1,0:T(8,128)(2,1)S(1)} %get-tuple-element.82.refs_2_, ...), custom_call_target="tpu_custom_call" | custom-call | flops 6000000000 | bytes 8000000 | tf_op jit(solution)/shard_map/front_2/pallas_call | solution.py:272
  105.4 4.2 %collective-permute-done.16.refs_11_ = bf16[4,27,48,128]{3,2,1,0:T(8,128)(2,1)S(1)} collective-permute-done((bf16[4,27,48,128]{3,2,1,0:T(8,128)(2,1)}, bf16[4,27,48,128]{3,2,1,0:T(8,128)(2,1)S(1)}, u32[]{:S(2)}, u32[]{:S(2)}) %collective-permute-start.16) | collective-permute-done | bytes 1327136 | tf_op jit(solution)/shard_map/ppermute | solution.py:716
  113.8 52.2 %middle.1 = (bf16[1024,768]{1,0:T(8,128)(2,1)}, f32[1024,768]{1,0:T(8,128)}, bf16[6,1024,128]{2,1,0:T(8,128)(2,1)}, bf16[4,4,16,48,128]{4,3,2,1,0:T(8,128)(2,1)}...) custom-call(s32[2]{0:T(128)} %copy-done.4, ...), custom_call_target="tpu_custom_call" | custom-call | flops 60000002048 | bytes 40000000 | tf_op jit(solution)/shard_map/middle/pallas_call | solution.py:463
  169.4 11.8 %back_0.1 = (bf16[6,1024,128]{2,1,0:T(8,128)(2,1)S(1)}, bf16[4,4,10,48,128]{4,3,2,1,0:T(8,128)(2,1)S(1)}, bf16[4,4,10,48,128]{4,3,2,1,0:T(8,128)(2,1)S(1)}, f32[8,768]{1,0:T(8,128)S(1)}) custom-call(s32[2]{0:T(128)S(1)} %copy-done.5, s32[1,2]{1,0:T(1,128)S(1)} %copy-done.3, bf16[6,1024,128]{2,1,0:T(8,128)(2,1)S(1)} %copy-done.12, ...), custom_call_target="tpu_custom_call" | custom-call | flops 17999998976 | bytes 8000000 | tf_op jit(solution)/shard_map/back_0/pallas_call | solution.py:634
  183.2 12.1 %back_1.1 = (bf16[6,1024,128]{2,1,0:T(8,128)(2,1)S(1)}, bf16[4,4,10,48,128]{4,3,2,1,0:T(8,128)(2,1)S(1)}, bf16[4,4,10,48,128]{4,3,2,1,0:T(8,128)(2,1)S(1)}, f32[8,768]{1,0:T(8,128)S(1)}) custom-call(s32[2]{0:T(128)S(1)} %copy-done.5, s32[1,2]{1,0:T(1,128)S(1)} %copy-done.3, ...), custom_call_target="tpu_custom_call", output_to_operand_aliasing={{1}: (8, {}), {2}: (9, {})} | custom-call | flops 17999998976 | bytes 8000000 | tf_op jit(solution)/shard_map/back_1/pallas_call | solution.py:634
  197.1 5.1 %collective-permute-done.23 = bf16[2,4,16,48,128]{4,3,2,1,0:T(8,128)(2,1)S(1)} collective-permute-done((bf16[2,4,16,48,128]{4,3,2,1,0:T(8,128)(2,1)S(1)}, bf16[2,4,16,48,128]{4,3,2,1,0:T(8,128)(2,1)S(1)}, u32[]{:S(2)}, u32[]{:S(2)}) %collective-permute-start.23) | collective-permute-done | bytes 1572896 | tf_op jit(solution)/shard_map/ppermute | solution.py:716
  202.5 14.6 %back_2.1 = (bf16[6,1024,128]{2,1,0:T(8,128)(2,1)S(1)}, bf16[4,4,10,48,128]{4,3,2,1,0:T(8,128)(2,1)S(1)}, bf16[4,4,10,48,128]{4,3,2,1,0:T(8,128)(2,1)S(1)}, f32[8,768]{1,0:T(8,128)}) custom-call(s32[2]{0:T(128)S(1)} %copy-done.5, s32[1,2]{1,0:T(1,128)S(1)} %copy-done.3, ...), custom_call_target="tpu_custom_call", output_to_operand_aliasing={{1}: (8, {}), {2}: (9, {})} | custom-call | flops 17999998976 | bytes 8000000 | tf_op jit(solution)/shard_map/back_2/pallas_call | solution.py:634
  219.5 3.8 %first_norm_back_0.1.refs_0_ = bf16[1024,768]{1,0:T(8,128)(2,1)} custom-call(bf16[1024,768]{1,0:T(8,128)(2,1)S(1)} %copy-done.1, bf16[6,1024,128]{2,1,0:T(8,128)(2,1)S(1)} %get-tuple-element.96.d_0, bf16[6,1024,128]{2,1,0:T(8,128)(2,1)S(1)} %get-tuple-element.107.d_1, bf16[6,1024,128]{2,1,0:T(8,128)(2,1)S(1)} %get-tuple-element.120.d_2, ...), custom_call_target="tpu_custom_call" | custom-call | flops 8000000000 | bytes 9000000 | tf_op jit(solution)/shard_map/first_norm_back_0/pallas_call | solution.py:682
  223.3 5.9 %collective-permute-done.26 = bf16[4,16,48,128]{3,2,1,0:T(8,128)(2,1)S(1)} collective-permute-done((bf16[4,16,48,128]{3,2,1,0:T(8,128)(2,1)S(1)}, bf16[4,16,48,128]{3,2,1,0:T(8,128)(2,1)S(1)}, u32[]{:S(2)}, u32[]{:S(2)}) %collective-permute-start.26) | collective-permute-done | bytes 786464 | tf_op jit(solution)/shard_map/ppermute | solution.py:716
  231.2 3.6 %collective-permute-start.32 = (bf16[16,48,128]{2,1,0:T(8,128)(2,1)S(1)}, bf16[16,48,128]{2,1,0:T(8,128)(2,1)S(1)}, u32[]{:S(2)}, u32[]{:S(2)}) collective-permute-start(bf16[16,48,128]{2,1,0:T(8,128)(2,1)S(1)} %get-tuple-element.140), channel_id=1, source_target_pairs={{0,24},{1,25},{2,26},{3,27},{4,28},{5,29},{6,30},{7,31},{8,16},{9,... | collective-permute-start | bytes 589832 | tf_op jit(solution)/shard_map/ppermute | solution.py:716
  234.9 3.8 %collective-permute-start.31 = (bf16[16,48,128]{2,1,0:T(8,128)(2,1)S(1)}, bf16[16,48,128]{2,1,0:T(8,128)(2,1)S(1)}, u32[]{:S(2)}, u32[]{:S(2)}) collective-permute-start(bf16[16,48,128]{2,1,0:T(8,128)(2,1)S(1)} %get-tuple-element.141), channel_id=1, source_target_pairs={{0,16},{1,17},{2,18},{3,19},{4,20},{5,21},{6,22},{7,23},{8,24},{9,... | collective-permute-start | bytes 589832 | tf_op jit(solution)/shard_map/ppermute | solution.py:716
  238.7 3.8 %first_norm_back_1.1 = bf16[1024,768]{1,0:T(8,128)(2,1)} custom-call(bf16[1024,768]{1,0:T(8,128)(2,1)S(1)} %copy-done.1, bf16[6,1024,128]{2,1,0:T(8,128)(2,1)S(1)} %get-tuple-element.96.d_0, bf16[6,1024,128]{2,1,0:T(8,128)(2,1)S(1)} %get-tuple-element.107.d_1, bf16[6,1024,128]{2,1,0:T(8,128)(2,1)S(1)} %get-tuple-element.120.d_2, ...), custom_call_target="tpu_custom_call", output_to_operand_aliasing={{}: (9, {})} | custom-call | flops 8000000000 | bytes 9000000 | tf_op jit(solution)/shard_map/first_norm_back_1/pallas_call | solution.py:682
  245.5 5.9 %collective-permute-done.31 = bf16[16,48,128]{2,1,0:T(8,128)(2,1)S(1)} collective-permute-done((bf16[16,48,128]{2,1,0:T(8,128)(2,1)S(1)}, bf16[16,48,128]{2,1,0:T(8,128)(2,1)S(1)}, u32[]{:S(2)}, u32[]{:S(2)}) %collective-permute-start.31) | collective-permute-done | bytes 196640 | tf_op jit(solution)/shard_map/ppermute | solution.py:716
  255.6 4.7 %collective-permute-start.33 = (bf16[10,48,128]{2,1,0:T(8,128)(2,1)S(1)}, bf16[10,48,128]{2,1,0:T(8,128)(2,1)S(1)}, u32[]{:S(2)}, u32[]{:S(2)}) collective-permute-start(bf16[10,48,128]{2,1,0:T(8,128)(2,1)S(1)} %get-tuple-element.148), channel_id=1, source_target_pairs={{0,8},{1,9},{2,10},{3,11},{4,12},{5,13},{6,14},{7,15},{8,0},{9,1},... | collective-permute-start | bytes 368648 | tf_op jit(solution)/shard_map/ppermute | solution.py:716
  263.2 5.5 %collective-permute-done.33 = bf16[10,48,128]{2,1,0:T(8,128)(2,1)S(1)} collective-permute-done((bf16[10,48,128]{2,1,0:T(8,128)(2,1)S(1)}, bf16[10,48,128]{2,1,0:T(8,128)(2,1)S(1)}, u32[]{:S(2)}, u32[]{:S(2)}) %collective-permute-start.33) | collective-permute-done | bytes 122912 | tf_op jit(solution)/shard_map/ppermute | solution.py:716
  268.9 6.8 %collective-permute-done.34 = bf16[10,48,128]{2,1,0:T(8,128)(2,1)S(1)} collective-permute-done((bf16[10,48,128]{2,1,0:T(8,128)(2,1)S(1)}, bf16[10,48,128]{2,1,0:T(8,128)(2,1)S(1)}, u32[]{:S(2)}, u32[]{:S(2)}) %collective-permute-start.34) | collective-permute-done | bytes 122912 | tf_op jit(solution)/shard_map/ppermute | solution.py:716
  (240 shorter events, 59.8 us)
Async XLA Ops:
  12.4 15.6 %collective-permute-start.2 = (bf16[27,48,128]{2,1,0:T(8,128)(2,1)S(1)}, bf16[27,48,128]{2,1,0:T(8,128)(2,1)S(1)}, u32[]{:S(2)}, u32[]{:S(2)}) collective-permute-start(bf16[27,48,128]{2,1,0:T(8,128)(2,1)S(1)} %constant_dynamic-update-slice_fusion), channel_id=1, source_target_pairs={{0,8},{1,9},{2,10},{3,11},{4,12},{5,13},{6,14},{7,15},{8,0},{9,1},... | collective-permute-start | bytes 995336 | tf_op jit(solution)/shard_map/ppermute | solution.py:716
  14.2 13.8 %collective-permute-start.6 = (bf16[10,48,128]{2,1,0:T(8,128)(2,1)S(1)}, bf16[10,48,128]{2,1,0:T(8,128)(2,1)S(1)}, u32[]{:S(2)}, u32[]{:S(2)}) collective-permute-start(bf16[10,48,128]{2,1,0:T(8,128)(2,1)S(1)} %constant_dynamic-update-slice_fusion.10), channel_id=1, source_target_pairs={{0,24},{1,25},{2,26},{3,27},{4,28},{5,29},{6,30},{7,31},{8,16},{9,... | collective-permute-start | bytes 368648 | tf_op jit(solution)/shard_map/ppermute | solution.py:716
  28.0 17.0 %collective-permute-start.7 = (bf16[4,10,48,128]{3,2,1,0:T(8,128)(2,1)S(1)}, bf16[4,10,48,128]{3,2,1,0:T(8,128)(2,1)S(1)}, u32[]{:S(2)}, u32[]{:S(2)}) collective-permute-start(bf16[4,10,48,128]{3,2,1,0:T(8,128)(2,1)S(1)} %pad_maximum_fusion.2.refs_3_.refs_4_), channel_id=1, source_target_pairs={{0,4},{1,3},{2,6},{3,1},{4,0},{5,7},{6,2},{7,5},{8,12},{9,11},{10,... | collective-permute-start | bytes 1474568 | tf_op jit(solution)/shard_map/ppermute | solution.py:716
  29.6 15.4 %collective-permute-start.3 = (bf16[27,48,128]{2,1,0:T(8,128)(2,1)S(1)}, bf16[27,48,128]{2,1,0:T(8,128)(2,1)S(1)}, u32[]{:S(2)}, u32[]{:S(2)}) collective-permute-start(bf16[27,48,128]{2,1,0:T(8,128)(2,1)S(1)} %constant_dynamic-update-slice_fusion), channel_id=1, source_target_pairs={{0,16},{1,17},{2,18},{3,19},{4,20},{5,21},{6,22},{7,23},{8,24},{9,... | collective-permute-start | bytes 995336 | tf_op jit(solution)/shard_map/ppermute | solution.py:716
  31.4 18.1 %collective-permute-start.9 = (bf16[4,10,48,128]{3,2,1,0:T(8,128)(2,1)S(1)}, bf16[4,10,48,128]{3,2,1,0:T(8,128)(2,1)S(1)}, u32[]{:S(2)}, u32[]{:S(2)}) collective-permute-start(bf16[4,10,48,128]{3,2,1,0:T(8,128)(2,1)S(1)} %pad_maximum_fusion.2.refs_3_.refs_4_), channel_id=1, source_target_pairs={{0,2},{1,5},{2,0},{3,7},{4,6},{5,1},{6,4},{7,3},{8,10},{9,13},{10,... | collective-permute-start | bytes 1474568 | tf_op jit(solution)/shard_map/ppermute | solution.py:716
  45.6 12.5 %collective-permute-start.4 = (bf16[27,48,128]{2,1,0:T(8,128)(2,1)}, bf16[27,48,128]{2,1,0:T(8,128)(2,1)S(1)}, u32[]{:S(2)}, u32[]{:S(2)}) collective-permute-start(bf16[27,48,128]{2,1,0:T(8,128)(2,1)} %copy-done.23), channel_id=1, source_target_pairs={{0,24},{1,25},{2,26},{3,27},{4,28},{5,29},{6,30},{7,31},{8,16},{9,... | collective-permute-start | bytes 995336 | tf_op jit(solution)/shard_map/ppermute | solution.py:716
  60.3 31.3 %collective-permute-start.14 = (bf16[4,27,48,128]{3,2,1,0:T(8,128)(2,1)}, bf16[4,27,48,128]{3,2,1,0:T(8,128)(2,1)}, u32[]{:S(2)}, u32[]{:S(2)}) collective-permute-start(bf16[4,27,48,128]{3,2,1,0:T(8,128)(2,1)} %pad_maximum_fusion.refs_8_), channel_id=1, source_target_pairs={{0,4},{1,3},{2,6},{3,1},{4,0},{5,7},{6,2},{7,5},{8,12},{9,11},{10,... | collective-permute-start | bytes 3981320 | tf_op jit(solution)/shard_map/ppermute | solution.py:716
  60.9 44.4 %collective-permute-start.15 = (bf16[4,27,48,128]{3,2,1,0:T(8,128)(2,1)}, bf16[4,27,48,128]{3,2,1,0:T(8,128)(2,1)S(1)}, u32[]{:S(2)}, u32[]{:S(2)}) collective-permute-start(bf16[4,27,48,128]{3,2,1,0:T(8,128)(2,1)} %pad_maximum_fusion.refs_8_), channel_id=1, source_target_pairs={{0,2},{1,5},{2,0},{3,7},{4,6},{5,1},{6,4},{7,3},{8,10},{9,13},{10,... | collective-permute-start | bytes 3981320 | tf_op jit(solution)/shard_map/ppermute | solution.py:716
  91.6 18.0 %collective-permute-start.16 = (bf16[4,27,48,128]{3,2,1,0:T(8,128)(2,1)}, bf16[4,27,48,128]{3,2,1,0:T(8,128)(2,1)S(1)}, u32[]{:S(2)}, u32[]{:S(2)}) collective-permute-start(bf16[4,27,48,128]{3,2,1,0:T(8,128)(2,1)} %collective-permute-done.14.refs_9_), channel_id=1, source_target_pairs={{0,2},{1,5},{2,0},{3,7},{4,6},{5,1},{6,4},{7,3},{8,10},{9,13},{10,... | collective-permute-start | bytes 3981320 | tf_op jit(solution)/shard_map/ppermute | solution.py:716
  93.0 16.6 %collective-permute-start.17 = (bf16[4,27,48,128]{3,2,1,0:T(8,128)(2,1)}, bf16[4,27,48,128]{3,2,1,0:T(8,128)(2,1)S(1)}, u32[]{:S(2)}, u32[]{:S(2)}) collective-permute-start(bf16[4,27,48,128]{3,2,1,0:T(8,128)(2,1)} %pad_maximum_fusion.refs_8_), channel_id=1, source_target_pairs={{0,1},{1,0},{2,3},{3,2},{4,5},{5,4},{6,7},{7,6},{8,9},{9,8},{10,11... | collective-permute-start | bytes 3981320 | tf_op jit(solution)/shard_map/ppermute | solution.py:716
  166.0 15.2 %collective-permute-start.21 = (bf16[4,4,16,48,128]{4,3,2,1,0:T(8,128)(2,1)}, bf16[4,4,16,48,128]{4,3,2,1,0:T(8,128)(2,1)S(1)}, u32[]{:S(2)}, u32[]{:S(2)}) collective-permute-start(bf16[4,4,16,48,128]{4,3,2,1,0:T(8,128)(2,1)} %get-tuple-element.99), channel_id=1, source_target_pairs={{0,1},{1,0},{2,3},{3,2},{4,5},{5,4},{6,7},{7,6},{8,9},{9,8},{10,11... | collective-permute-start | bytes 9437192 | tf_op jit(solution)/shard_map/ppermute | solution.py:716
  166.2 16.9 %collective-permute-start.22 = (bf16[4,4,11,48,128]{4,3,2,1,0:T(8,128)(2,1)}, bf16[4,4,11,48,128]{4,3,2,1,0:T(8,128)(2,1)S(1)}, u32[]{:S(2)}, u32[]{:S(2)}) collective-permute-start(bf16[4,4,11,48,128]{4,3,2,1,0:T(8,128)(2,1)} %get-tuple-element.101), channel_id=1, source_target_pairs={{0,1},{1,0},{2,3},{3,2},{4,5},{5,4},{6,7},{7,6},{8,9},{9,8},{10,11... | collective-permute-start | bytes 6488072 | tf_op jit(solution)/shard_map/ppermute | solution.py:716
  181.7 20.5 %collective-permute-start.23 = (bf16[2,4,16,48,128]{4,3,2,1,0:T(8,128)(2,1)S(1)}, bf16[2,4,16,48,128]{4,3,2,1,0:T(8,128)(2,1)S(1)}, u32[]{:S(2)}, u32[]{:S(2)}) collective-permute-start(bf16[2,4,16,48,128]{4,3,2,1,0:T(8,128)(2,1)S(1)} %add_convert_fusion), channel_id=1, source_target_pairs={{0,2},{1,5},{2,0},{3,7},{4,6},{5,1},{6,4},{7,3},{8,10},{9,13},{10,... | collective-permute-start | bytes 4718600 | tf_op jit(solution)/shard_map/ppermute | solution.py:716
  195.6 21.9 %collective-permute-start.24 = (bf16[2,4,11,48,128]{4,3,2,1,0:T(8,128)(2,1)S(1)}, bf16[2,4,11,48,128]{4,3,2,1,0:T(8,128)(2,1)S(1)}, u32[]{:S(2)}, u32[]{:S(2)}) collective-permute-start(bf16[2,4,11,48,128]{4,3,2,1,0:T(8,128)(2,1)S(1)} %add_convert_fusion.1), channel_id=1, source_target_pairs={{0,2},{1,5},{2,0},{3,7},{4,6},{5,1},{6,4},{7,3},{8,10},{9,13},{10,... | collective-permute-start | bytes 3244040 | tf_op jit(solution)/shard_map/ppermute | solution.py:716
  217.7 33.9 %collective-permute-start.29 = (bf16[4,11,48,128]{3,2,1,0:T(8,128)(2,1)S(1)}, bf16[4,11,48,128]{3,2,1,0:T(8,128)(2,1)S(1)}, u32[]{:S(2)}, u32[]{:S(2)}) collective-permute-start(bf16[4,11,48,128]{3,2,1,0:T(8,128)(2,1)S(1)} %fusion.1), channel_id=1, source_target_pairs={{0,4},{1,3},{2,6},{3,1},{4,0},{5,7},{6,2},{7,5},{8,12},{9,11},{10,... | collective-permute-start | bytes 1622024 | tf_op jit(solution)/shard_map/ppermute | solution.py:716
  229.5 15.5 %collective-permute-start.27 = (bf16[2,4,10,48,128]{4,3,2,1,0:T(8,128)(2,1)S(1)}, bf16[2,4,10,48,128]{4,3,2,1,0:T(8,128)(2,1)S(1)}, u32[]{:S(2)}, u32[]{:S(2)}) collective-permute-start(bf16[2,4,10,48,128]{4,3,2,1,0:T(8,128)(2,1)S(1)} %add_convert_fusion.2), channel_id=1, source_target_pairs={{0,2},{1,5},{2,0},{3,7},{4,6},{5,1},{6,4},{7,3},{8,10},{9,13},{10,... | collective-permute-start | bytes 2949128 | tf_op jit(solution)/shard_map/ppermute | solution.py:716
  231.2 14.3 %collective-permute-start.32 = (bf16[16,48,128]{2,1,0:T(8,128)(2,1)S(1)}, bf16[16,48,128]{2,1,0:T(8,128)(2,1)S(1)}, u32[]{:S(2)}, u32[]{:S(2)}) collective-permute-start(bf16[16,48,128]{2,1,0:T(8,128)(2,1)S(1)} %get-tuple-element.140), channel_id=1, source_target_pairs={{0,24},{1,25},{2,26},{3,27},{4,28},{5,29},{6,30},{7,31},{8,16},{9,... | collective-permute-start | bytes 589832 | tf_op jit(solution)/shard_map/ppermute | solution.py:716
  234.9 16.6 %collective-permute-start.31 = (bf16[16,48,128]{2,1,0:T(8,128)(2,1)S(1)}, bf16[16,48,128]{2,1,0:T(8,128)(2,1)S(1)}, u32[]{:S(2)}, u32[]{:S(2)}) collective-permute-start(bf16[16,48,128]{2,1,0:T(8,128)(2,1)S(1)} %get-tuple-element.141), channel_id=1, source_target_pairs={{0,16},{1,17},{2,18},{3,19},{4,20},{5,21},{6,22},{7,23},{8,24},{9,... | collective-permute-start | bytes 589832 | tf_op jit(solution)/shard_map/ppermute | solution.py:716
  238.7 12.8 %collective-permute-start.30 = (bf16[16,48,128]{2,1,0:T(8,128)(2,1)S(1)}, bf16[16,48,128]{2,1,0:T(8,128)(2,1)S(1)}, u32[]{:S(2)}, u32[]{:S(2)}) collective-permute-start(bf16[16,48,128]{2,1,0:T(8,128)(2,1)S(1)} %get-tuple-element.142), channel_id=1, source_target_pairs={{0,8},{1,9},{2,10},{3,11},{4,12},{5,13},{6,14},{7,15},{8,0},{9,1},... | collective-permute-start | bytes 589832 | tf_op jit(solution)/shard_map/ppermute | solution.py:716
  251.8 16.9 %collective-permute-start.37 = (bf16[11,48,128]{2,1,0:T(8,128)(2,1)S(1)}, bf16[11,48,128]{2,1,0:T(8,128)(2,1)S(1)}, u32[]{:S(2)}, u32[]{:S(2)}) collective-permute-start(bf16[11,48,128]{2,1,0:T(8,128)(2,1)S(1)} %get-tuple-element.143), channel_id=1, source_target_pairs={{0,16},{1,17},{2,18},{3,19},{4,20},{5,21},{6,22},{7,23},{8,24},{9,... | collective-permute-start | bytes 405512 | tf_op jit(solution)/shard_map/ppermute | solution.py:716
  254.9 13.9 %collective-permute-start.36 = (bf16[11,48,128]{2,1,0:T(8,128)(2,1)S(1)}, bf16[11,48,128]{2,1,0:T(8,128)(2,1)S(1)}, u32[]{:S(2)}, u32[]{:S(2)}) collective-permute-start(bf16[11,48,128]{2,1,0:T(8,128)(2,1)S(1)} %get-tuple-element.145), channel_id=1, source_target_pairs={{0,8},{1,9},{2,10},{3,11},{4,12},{5,13},{6,14},{7,15},{8,0},{9,1},... | collective-permute-start | bytes 405512 | tf_op jit(solution)/shard_map/ppermute | solution.py:716
  255.6 13.1 %collective-permute-start.33 = (bf16[10,48,128]{2,1,0:T(8,128)(2,1)S(1)}, bf16[10,48,128]{2,1,0:T(8,128)(2,1)S(1)}, u32[]{:S(2)}, u32[]{:S(2)}) collective-permute-start(bf16[10,48,128]{2,1,0:T(8,128)(2,1)S(1)} %get-tuple-element.148), channel_id=1, source_target_pairs={{0,8},{1,9},{2,10},{3,11},{4,12},{5,13},{6,14},{7,15},{8,0},{9,1},... | collective-permute-start | bytes 368648 | tf_op jit(solution)/shard_map/ppermute | solution.py:716
  260.3 15.3 %collective-permute-start.34 = (bf16[10,48,128]{2,1,0:T(8,128)(2,1)S(1)}, bf16[10,48,128]{2,1,0:T(8,128)(2,1)S(1)}, u32[]{:S(2)}, u32[]{:S(2)}) collective-permute-start(bf16[10,48,128]{2,1,0:T(8,128)(2,1)S(1)} %get-tuple-element.146), channel_id=1, source_target_pairs={{0,16},{1,17},{2,18},{3,19},{4,20},{5,21},{6,22},{7,23},{8,24},{9,... | collective-permute-start | bytes 368648 | tf_op jit(solution)/shard_map/ppermute | solution.py:716
  262.3 13.4 %collective-permute-start.35 = (bf16[10,48,128]{2,1,0:T(8,128)(2,1)S(1)}, bf16[10,48,128]{2,1,0:T(8,128)(2,1)S(1)}, u32[]{:S(2)}, u32[]{:S(2)}) collective-permute-start(bf16[10,48,128]{2,1,0:T(8,128)(2,1)S(1)} %get-tuple-element.147), channel_id=1, source_target_pairs={{0,24},{1,25},{2,26},{3,27},{4,28},{5,29},{6,30},{7,31},{8,16},{9,... | collective-permute-start | bytes 368648 | tf_op jit(solution)/shard_map/ppermute | solution.py:716
  (56 other events, 635.7 us)
